TPU v7x, 32 devices: a whole 2x2x4 slice. The times are simulated.
32 devices in a mesh: seq: 8 (over z, y), head: 4 (over x, core).
Axes of the slice: x: 2, y: 2, z: 4, core: 2. Of those that a mesh axis runs over, the one named last changes fastest.
Arguments:
- queries: bfloat16 [8192, 512], P('seq', 'head'), may hold values from -6 to 6
- keys: bfloat16 [8192, 512], P('seq', 'head'), may hold values from -6 to 6
- values: bfloat16 [8192, 512], P('seq', 'head'), may hold values from -6 to 6
- out_grad: bfloat16 [8192, 512], P('seq', 'head'), may hold values from -6 to 6
- lengths: int32 [4], replicated, may hold values from 1 to 3072, 8192 in all
- w_proj: bfloat16 [3, 512, 512], P(None, None, 'head'), may hold values from -0.25 to 0.25
Outputs:
- d_input: float32 [8192, 512], P(('seq', 'head'))
Inputs may be any that keep to these rules, and one draw needn't show every extreme that they name: The lengths sum to 8192; the longest is exactly 3072.
All inputs are finite; a program needn't handle non-finite values.
Results may differ from a plain program's by a relative error of at most 0.006.
Values may be sent and summed in bfloat16 or wider, within the bound.
No kernel may reach another device: no remote copies, remote signals or barrier semaphores. Data moves between devices by JAX's collectives and lax.ppermute only.
A program may use at most 64 MiB of HBM per device.

v0:
```python
import math

import jax
import jax.numpy as jnp
from jax import lax
from jax.experimental import pallas as pl
from jax.experimental.pallas import tpu as pltpu
from jax.sharding import PartitionSpec as P


MAXLEN = 3072
F32 = jnp.float32
BF16 = jnp.bfloat16
VMEM = pl.BlockSpec(memory_space=pltpu.VMEM)
SMEM = pl.BlockSpec(memory_space=pltpu.SMEM)


def shift(value, by, flip=0):
    tiles, heads = lax.axis_size("seq"), lax.axis_size("head")
    pairs = [
        (t * heads + h, (t + by) * heads + (h ^ flip))
        for t in range(tiles)
        for h in range(heads)
        if 0 <= t + by < tiles
    ]
    return lax.ppermute(value, ("seq", "head"), pairs)


def user_bounds(lengths_ref, position):
    def step(u, carry):
        end, first, last = carry
        end = end + lengths_ref[u]
        past = end <= position
        return (
            end,
            jnp.where(past, end, first),
            jnp.where(past, last, jnp.minimum(last, end)),
        )

    zero = jnp.int32(0)
    _, first, last = lax.fori_loop(
        0, lengths_ref.shape[0], step, (zero, zero, jnp.int32(2**30))
    )
    return first, last


def pair_limits(lengths_ref, query_start, key_start, rows):
    first, last = user_bounds(lengths_ref, query_start)
    live = first <= key_start + rows - 1
    query_rows = jnp.where(live, jnp.minimum(last - query_start, rows), 0)
    key_row = jnp.maximum(first - key_start, 0)
    return query_rows, key_row


def scores(q, g, k, v, mask=None):
    nt = (((1,), (1,)), ((), ()))
    half = lax.dot_general(k, q, nt, preferred_element_type=F32) * (0.5 * q.shape[1] ** -0.5)
    da = lax.dot_general(v, g, nt, preferred_element_type=F32)
    gate = 1.0 + jnp.tanh(half)
    if mask is not None:
        gate = jnp.where(mask, gate, 0.0)
    a = half * gate
    f = (gate + a * (2.0 - gate)) * da
    return a.astype(BF16), f.astype(BF16)


def add_block(qs, ks, q, g, k, a, f, dq_ref, dk_ref, dv_ref):
    dv_ref[ks, :] += jnp.dot(a, g, preferred_element_type=F32)
    dk_ref[ks, :] += jnp.dot(f, q, preferred_element_type=F32)
    dq_ref[qs, :] += lax.dot_general(f, k, (((0,), (0,)), ((), ())), preferred_element_type=F32)


def copy_rows(out_ref, ref, start, low, high):
    block, width = out_ref.shape[1:]
    src = pl.ds(start, block)
    inside = (low <= 0) & (high >= block)

    @pl.when(inside)
    def _():
        for n in range(2):
            out_ref[n] = ref[n, src, :]

    @pl.when(jnp.logical_not(inside))
    def _():
        row = lax.broadcasted_iota(jnp.int32, (block, width), 0)
        kept = (row >= low) & (row < high)
        for n in range(2):
            out_ref[n] = jnp.where(kept, ref[n, src, :], jnp.zeros((), BF16))


def sweep(
    qg_ref, kv_ref, dq_ref, dk_ref, dv_ref, query_rows, key_row, key_blocks, qm_ref, km_ref
):
    block = qg_ref.shape[1]
    everything = pl.ds(0, block)

    @pl.when(query_rows > 0)
    def _():
        copy_rows(qm_ref, qg_ref, 0, 0, query_rows)

        def key_block(kb, carry):
            off = pl.multiple_of(kb * block, block)
            ks = pl.ds(off, block)
            copy_rows(km_ref, kv_ref, off, key_row - off, block)
            q, g, k, v = qm_ref[0], qm_ref[1], km_ref[0], km_ref[1]
            a, f = scores(q, g, k, v)
            add_block(everything, ks, q, g, k, a, f, dq_ref, dk_ref, dv_ref)
            return carry

        lax.fori_loop(key_row // block, key_blocks, key_block, 0)


def halves(ref):
    half = ref.shape[0] // 2
    return ref.at[pl.ds(0, half)], ref.at[pl.ds(half, half)]


def pack_kernel(q_hbm, g_hbm, k_hbm, v_hbm, qa_ref, qb_ref, kv_ref, sems):
    half = qa_ref.shape[1]
    copies = [
        pltpu.make_async_copy(k_hbm, kv_ref.at[0], sems.at[0]),
        pltpu.make_async_copy(v_hbm, kv_ref.at[1], sems.at[1]),
    ]
    for n, ref in enumerate((qa_ref, qb_ref)):
        for m, hbm in enumerate((q_hbm, g_hbm)):
            part = hbm.at[pl.ds(n * half, half)]
            copies.append(pltpu.make_async_copy(part, ref.at[m], sems.at[2 + 2 * n + m]))
    for copy in copies:
        copy.start()
    for copy in copies:
        copy.wait()


def own_kernel(lengths_ref, qa_ref, qb_ref, kv_ref, dq_ref, dk_ref, dv_ref, *masked):
    block = qa_ref.shape[1]
    strip = block // 2
    start = lax.axis_index("seq") * (2 * block)
    dq_ref[...] = jnp.zeros_like(dq_ref)
    dk_ref[...] = jnp.zeros_like(dk_ref)
    dv_ref[...] = jnp.zeros_like(dv_ref)

    for b, qg_ref in enumerate((qa_ref, qb_ref)):
        query = lax.broadcasted_iota(jnp.int32, (1, block), 1) + start + b * block

        def step(u, carry):
            end, first = carry
            end = end + lengths_ref[u]
            return end, jnp.where(end <= query, end, first)

        _, first = lax.fori_loop(
            0, lengths_ref.shape[0], step, (jnp.int32(0), jnp.zeros((1, block), jnp.int32))
        )
        for off in range(0, block, strip):
            ks, qs = pl.ds(b * block + off, strip), pl.ds(b * block + off, block - off)
            key = lax.broadcasted_iota(jnp.int32, (strip, block - off), 0) + start + b * block + off
            mask = (key <= query[:, off:]) & (key >= first[:, off:])
            q, g = qg_ref[0, off:, :], qg_ref[1, off:, :]
            k, v = kv_ref[0, ks, :], kv_ref[1, ks, :]
            a, f = scores(q, g, k, v, mask)
            add_block(qs, ks, q, g, k, a, f, dq_ref, dk_ref, dv_ref)

    query_rows, key_row = pair_limits(lengths_ref, start + block, start, block)
    sweep(qb_ref, kv_ref, halves(dq_ref)[1], dk_ref, dv_ref, query_rows, key_row, 1, *masked)


def next_kernel(
    lengths_ref, qan_ref, kv_ref, dk_in, dv_in, dqn_ref, dk_ref, dv_ref, *masked
):
    rows = kv_ref.shape[1]
    me = lax.axis_index("seq")
    dqn_ref[...] = jnp.zeros_like(dqn_ref)
    query_rows, key_row = pair_limits(lengths_ref, (me + 1) * rows, me * rows, rows)
    sweep(qan_ref, kv_ref, dqn_ref, dk_ref, dv_ref, query_rows, key_row, 2, *masked)


def near_kernel(
    lengths_ref, qa_ref, qb_ref, kvn_ref, dq_in, dq_ref, dkn_ref, dvn_ref, *masked
):
    half, rows = qa_ref.shape[1], kvn_ref.shape[1]
    me = lax.axis_index("seq")
    dkn_ref[...] = jnp.zeros_like(dkn_ref)
    dvn_ref[...] = jnp.zeros_like(dvn_ref)
    query_rows, key_row = pair_limits(lengths_ref, me * rows, (me - 2) * rows, rows)
    for n, (qg_ref, dq) in enumerate(zip((qa_ref, qb_ref), halves(dq_ref))):
        sweep(qg_ref, kvn_ref, dq, dkn_ref, dvn_ref, query_rows - n * half, key_row, 2, *masked)


def rest_kernel(
    lengths_ref, qan_ref, qbn_ref, kv_ref, kvn_ref,
    dq_ref, dqa_in, dk_in, dv_in, dkn_in, dvn_in,
    keep_ref, send_ref, dq_same, dq_cross, dkv_same, dkv_cross,
    dqa_ref, dk_own, dv_own, dk_ref, dv_ref,
    dqb_ref, *masked,
):
    width = dq_ref.shape[1]
    rows = kv_ref.shape[1]
    me = lax.axis_index("seq")
    dqb_ref[...] = jnp.zeros_like(dqb_ref)
    query_rows, key_row = pair_limits(lengths_ref, (me + 1) * rows, me * rows, rows)
    tail_rows = query_rows - rows // 2
    sweep(qbn_ref, kv_ref, dqb_ref, dk_own, dv_own, tail_rows, key_row, 2, *masked)
    query_rows, key_row = pair_limits(lengths_ref, (me + 1) * rows, (me - 2) * rows, rows)
    tail_rows = query_rows - rows // 2
    sweep(qan_ref, kvn_ref, dqa_ref, dk_ref, dv_ref, query_rows, key_row, 2, *masked)
    sweep(qbn_ref, kvn_ref, dqb_ref, dk_ref, dv_ref, tail_rows, key_row, 2, *masked)

    norm = MAXLEN**-0.5
    inner = 0.5 * norm * width**-0.5
    half = dq_same.shape[0]
    block = half // 2
    head = lax.axis_index("head")
    high, low = head // 2, head % 2
    for bit, dq_out, dkv_out in ((high, dq_same, dkv_same), (1 - high, dq_cross, dkv_cross)):
        src = pl.ds(pl.multiple_of(bit * half, half), half)
        dq_out[...] = (jnp.where(bit == 0, dqa_ref[...], dqb_ref[...]) * inner).astype(BF16)
        dkv_out[0] = (dk_ref[src, :] * inner).astype(BF16)
        dkv_out[1] = (dv_ref[src, :] * norm).astype(BF16)
    for bit, out_ref in ((low, keep_ref), (1 - low, send_ref)):
        for top in range(2):
            src = pl.ds(pl.multiple_of((2 * top + bit) * block, block), block)
            dst = pl.ds(top * block, block)
            own = (dq_ref[src, :] * inner, dk_own[src, :] * inner, dv_own[src, :] * norm)
            for c, part in enumerate(own):
                out_ref[c, dst, :] = part.astype(BF16)


def project(grads, weights):
    return lax.dot_general(
        jnp.concatenate(grads, axis=1), jnp.concatenate(weights, axis=1),
        (((1,), (1,)), ((), ())), preferred_element_type=F32,
    )


def local_kernel(keep_ref, got_ref, w_ref, w1_ref, mine_ref, send_ref):
    block = mine_ref.shape[0]
    high = lax.axis_index("head") // 2
    weights = [ref[c] for ref in (w_ref, w1_ref) for c in range(3)]
    for bit, out_ref in ((1 - high, send_ref), (high, mine_ref)):
        src = pl.ds(pl.multiple_of(bit * block, block), block)
        grads = [ref[c, src, :] for ref in (keep_ref, got_ref) for c in range(3)]
        out_ref[...] = project(grads, weights).astype(out_ref.dtype)


def split_kernel(dq_same, dkv_same, dq_cross, dkv_cross, keep_ref, send_ref):
    block = keep_ref.shape[2]
    low = lax.axis_index("head") % 2
    for bit, out_ref in ((1 - low, send_ref), (low, keep_ref)):
        src = pl.ds(pl.multiple_of(bit * block, block), block)
        for n, (dq, dkv) in enumerate(((dq_same, dkv_same), (dq_cross, dkv_cross))):
            out_ref[n, 0] = dq[src, :]
            out_ref[n, 1] = dkv[0, src, :]
            out_ref[n, 2] = dkv[1, src, :]


def final_kernel(keep_ref, got_ref, mine_ref, arrived_ref, w_ref, w1_ref, w2_ref, w3_ref, out_ref):
    grads, weights = [], []
    for half_ref, pair in ((keep_ref, (w_ref, w2_ref)), (got_ref, (w1_ref, w3_ref))):
        for n, weight in enumerate(pair):
            grads += [half_ref[n, c] for c in range(3)]
            weights += [weight[c] for c in range(3)]
    out_ref[...] = project(grads, weights) + mine_ref[...] + arrived_ref[...].astype(F32)


def call(body, outs, args, flops, scratch=(), lengths=True, space=VMEM, aliases=()):
    specs = [SMEM if lengths and n == 0 else space for n in range(len(args))]
    moved = sum(math.prod(a.shape) * a.dtype.itemsize for a in (*args, *outs))
    return pl.pallas_call(
        body,
        out_shape=outs,
        in_specs=specs,
        out_specs=tuple(VMEM for _ in outs),
        scratch_shapes=scratch,
        input_output_aliases=dict(aliases),
        compiler_params=pltpu.CompilerParams(vmem_limit_bytes=24 * 2**20),
        cost_estimate=pl.CostEstimate(flops=flops, bytes_accessed=moved, transcendentals=0),
    )(*args)


def shards(queries, keys, values, out_grad, lengths, w_proj):
    rows, width = queries.shape
    model = w_proj.shape[1]
    heads = lax.axis_size("head")
    block = rows // heads
    like = jax.ShapeDtypeStruct
    wide = like((rows, width), F32)
    pair_flops = 10 * rows * rows * width

    half = like((2, rows // 2, width), BF16)
    half_wide = like((rows // 2, width), F32)
    inputs = (queries, out_grad, keys, values)
    qa, qb, kv = call(
        pack_kernel, (half, half, like((2, rows, width), BF16)),
        tuple(pltpu.with_memory_space_constraint(x, pltpu.HBM) for x in inputs), 1000,
        scratch=[pltpu.SemaphoreType.DMA((6,))], lengths=False,
        space=pl.BlockSpec(memory_space=pltpu.HBM),
    )
    kvn = shift(kv, 2)
    qan = shift(qa, -1)
    qbn = shift(qb, -1)
    w2 = shift(w_proj, 0, 2)

    masked = [pltpu.VMEM((2, rows // 2, width), BF16)] * 2
    dq, dk, dv = call(
        own_kernel, (wide, wide, wide), (lengths, qa, qb, kv), pair_flops, scratch=masked
    )
    dqn, dk, dv = call(
        next_kernel, (half_wide, wide, wide), (lengths, qan, kv, dk, dv), pair_flops,
        scratch=masked, aliases=((3, 1), (4, 2)),
    )
    dq, dkn, dvn = call(
        near_kernel, (wide, wide, wide), (lengths, qa, qb, kvn, dq), pair_flops,
        scratch=masked, aliases=((4, 0),),
    )
    keep, send, dq_same, dq_cross, dkv_same, dkv_cross, *_ = call(
        rest_kernel,
        (
            like((3, 2 * block, width), BF16), like((3, 2 * block, width), BF16),
            like((2 * block, width), BF16), like((2 * block, width), BF16),
            like((2, 2 * block, width), BF16), like((2, 2 * block, width), BF16),
            half_wide, wide, wide, wide, wide,
        ),
        (lengths, qan, qbn, kv, kvn, dq, dqn, dk, dv, dkn, dvn), pair_flops,
        scratch=[pltpu.VMEM((rows // 2, width), F32), *masked],
        aliases=((6, 6), (7, 7), (8, 8), (9, 9), (10, 10)),
    )
    w1, w3 = shift(w_proj, 0, 1), shift(w2, 0, 1)
    dkv_cross = shift(dkv_cross, -2, 2)
    dkv_same = shift(dkv_same, -2)
    dq_cross = shift(dq_cross, 1, 2)
    dq_same = shift(dq_same, 1)
    got = shift(send, 0, 1)
    mine, send = call(
        local_kernel, (like((block, model), F32), like((block, model), BF16)),
        (keep, got, w_proj, w1), 12 * block * width * model, lengths=False,
    )
    arrived = shift(send, 0, 2)

    quarter = like((2, 3, block, width), BF16)
    keep, send = call(
        split_kernel, (quarter, quarter), (dq_same, dkv_same, dq_cross, dkv_cross), 1000,
        lengths=False,
    )
    got = shift(send, 0, 1)
    (out,) = call(
        final_kernel, (like((block, model), F32),),
        (keep, got, mine, arrived, w_proj, w1, w2, w3), 24 * block * width * model, lengths=False,
    )
    return out


def solution(mesh):
    return jax.shard_map(
        shards,
        mesh=mesh,
        in_specs=(
            P("seq", "head"),
            P("seq", "head"),
            P("seq", "head"),
            P("seq", "head"),
            P(),
            P(None, None, "head"),
        ),
        out_specs=P(("seq", "head"), None),
        check_vma=False,
    )
```

profile of v0, /device:TPU:0, one launch (start us, length us, event | category | flops | bytes accessed | tf_op | source)
XLA Modules:
  0.0 56.9 jit_solution(1961741951679785693)
XLA Ops:
  0.0 0.0 copy-start
  0.0 1.3 %shard_map.64 = (bf16[2,512,128]{2,1,0:T(8,128)(2,1)S(1)}, bf16[2,512,128]{2,1,0:T(8,128)(2,1)S(1)}, bf16[2,1024,128]{2,1,0:T(8,128)(2,1)S(1)}) custom-call(bf16[1024,128]{1,0:T(8,128)(2,1)} %q_hbm.1, bf16[1024,128]{1,0:T(8,128)(2,1)} %g_hbm.1, bf16[1024,128]{1,0:T(8,128)(2,1)} %k_hbm.1, bf16[1024,128]{1,0:T(8,128)(2,1)} %v_hbm.1), custom_call_target="tpu_custom_call" | custom-call | flops 1000 | bytes 2097152 | tf_op jit(solution)/shard_map/pallas_call | solution.py:267
  1.3 5.0 %collective-permute-start.2 = (bf16[2,1024,128]{2,1,0:T(8,128)(2,1)S(1)}, bf16[2,1024,128]{2,1,0:T(8,128)(2,1)S(1)}, u32[]{:S(2)}, u32[]{:S(2)}) collective-permute-start(bf16[2,1024,128]{2,1,0:T(8,128)(2,1)S(1)} %get-tuple-element.29.kv_ref), channel_id=1, source_target_pairs={{0,8},{1,9},{2,10},{3,11},{4,12},{5,13},{6,14},{7,15},{8,16},{9,17... | collective-permute-start | bytes 1572872 | tf_op jit(solution)/shard_map/ppermute | solution.py:26
  6.3 0.0 copy-start.1
  6.3 1.3 %collective-permute-start = (bf16[2,512,128]{2,1,0:T(8,128)(2,1)S(1)}, bf16[2,512,128]{2,1,0:T(8,128)(2,1)S(1)}, u32[]{:S(2)}, u32[]{:S(2)}) collective-permute-start(bf16[2,512,128]{2,1,0:T(8,128)(2,1)S(1)} %get-tuple-element.27.qa_ref), channel_id=1, source_target_pairs={{4,0},{5,1},{6,2},{7,3},{8,4},{9,5},{10,6},{11,7},{12,8},{13,9},{1... | collective-permute-start | bytes 786440 | tf_op jit(solution)/shard_map/ppermute | solution.py:26
  7.6 0.0 copy-done
  7.6 0.1 collective-permute-start.9
  7.7 1.6 %collective-permute-start.11 = (bf16[3,512,128]{2,1,0:T(8,128)(2,1)S(1)}, bf16[3,512,128]{2,1,0:T(8,128)(2,1)S(1)}, u32[]{:S(2)}, u32[]{:S(2)}) collective-permute-start(bf16[3,512,128]{2,1,0:T(8,128)(2,1)S(1)} %copy-done), channel_id=1, source_target_pairs={{0,2},{1,3},{2,0},{3,1},{4,6},{5,7},{6,4},{7,5},{8,10},{9,11},{10,... | collective-permute-start | bytes 1179656 | tf_op jit(solution)/shard_map/ppermute | solution.py:26
  9.2 1.3 %collective-permute-start.1 = (bf16[2,512,128]{2,1,0:T(8,128)(2,1)S(1)}, bf16[2,512,128]{2,1,0:T(8,128)(2,1)S(1)}, u32[]{:S(2)}, u32[]{:S(2)}) collective-permute-start(bf16[2,512,128]{2,1,0:T(8,128)(2,1)S(1)} %get-tuple-element.28.qb_ref), channel_id=1, source_target_pairs={{4,0},{5,1},{6,2},{7,3},{8,4},{9,5},{10,6},{11,7},{12,8},{13,9},{1... | collective-permute-start | bytes 786440 | tf_op jit(solution)/shard_map/ppermute | solution.py:26
  10.5 0.0 copy-done.1
  10.5 3.8 %shard_map.65 = (f32[1024,128]{1,0:T(8,128)S(1)}, f32[1024,128]{1,0:T(8,128)S(1)}, f32[1024,128]{1,0:T(8,128)S(1)}) custom-call(s32[4]{0:T(128)S(1)} %copy-done.1, bf16[2,512,128]{2,1,0:T(8,128)(2,1)S(1)} %get-tuple-element.27.qa_ref, bf16[2,512,128]{2,1,0:T(8,128)(2,1)S(1)} %get-tuple-element.28.qb_ref, bf16[2,1024,128]{2,1,0:T(8,128)(2,1)S(1)} %get-tuple-element.29.kv_ref), custom_call_target="tpu_custom_call" | custom-call | flops 1342177280 | bytes 2621456 | tf_op jit(solution)/shard_map/pallas_call | solution.py:267
  14.3 2.8 %collective-permute-done.qan_ref = bf16[2,512,128]{2,1,0:T(8,128)(2,1)S(1)} collective-permute-done((bf16[2,512,128]{2,1,0:T(8,128)(2,1)S(1)}, bf16[2,512,128]{2,1,0:T(8,128)(2,1)S(1)}, u32[]{:S(2)}, u32[]{:S(2)}) %collective-permute-start) | collective-permute-done | bytes 262176 | tf_op jit(solution)/shard_map/ppermute | solution.py:26
  17.1 2.7 %shard_map.67 = (f32[512,128]{1,0:T(8,128)S(1)}, f32[1024,128]{1,0:T(8,128)S(1)}, f32[1024,128]{1,0:T(8,128)S(1)}) custom-call(s32[4]{0:T(128)S(1)} %copy-done.1, bf16[2,512,128]{2,1,0:T(8,128)(2,1)S(1)} %collective-permute-done.qan_ref, bf16[2,1024,128]{2,1,0:T(8,128)(2,1)S(1)} %get-tuple-element.29.kv_ref, ...), custom_call_target="tpu_custom_call", output_to_operand_aliasing={{1}: (3, {}), {2}: (4, {})} | custom-call | flops 1342177280 | bytes 3145744 | tf_op jit(solution)/shard_map/pallas_call | solution.py:267
  19.8 0.0 collective-permute-done.2.kvn_ref
  19.8 0.7 %shard_map.66 = (f32[1024,128]{1,0:T(8,128)S(1)}, f32[1024,128]{1,0:T(8,128)S(1)}, f32[1024,128]{1,0:T(8,128)S(1)}) custom-call(s32[4]{0:T(128)S(1)} %copy-done.1, bf16[2,512,128]{2,1,0:T(8,128)(2,1)S(1)} %get-tuple-element.27.qa_ref, bf16[2,512,128]{2,1,0:T(8,128)(2,1)S(1)} %get-tuple-element.28.qb_ref, ...), custom_call_target="tpu_custom_call", output_to_operand_aliasing={{0}: (4, {})} | custom-call | flops 1342177280 | bytes 3145744 | tf_op jit(solution)/shard_map/pallas_call | solution.py:267
  20.5 1.1 %collective-permute-done.1.qbn_ref = bf16[2,512,128]{2,1,0:T(8,128)(2,1)S(1)} collective-permute-done((bf16[2,512,128]{2,1,0:T(8,128)(2,1)S(1)}, bf16[2,512,128]{2,1,0:T(8,128)(2,1)S(1)}, u32[]{:S(2)}, u32[]{:S(2)}) %collective-permute-start.1) | collective-permute-done | bytes 262176 | tf_op jit(solution)/shard_map/ppermute | solution.py:26
  21.6 3.0 %shard_map.68 = (bf16[3,512,128]{2,1,0:T(8,128)(2,1)S(1)}, bf16[3,512,128]{2,1,0:T(8,128)(2,1)S(1)}, bf16[512,128]{1,0:T(8,128)(2,1)S(1)}, bf16[512,128]{1,0:T(8...) custom-call(s32[4]{0:T(128)S(1)} %copy-done.1, ...), custom_call_target="tpu_custom_call", output_to_operand_aliasing={{6}: (6, {}), {7}: (7, {}), {8}: (8, {}), {9}: (9, {}), {10... | custom-call | flops 1342177280 | bytes 8388624 | tf_op jit(solution)/shard_map/pallas_call | solution.py:267
  24.6 0.1 collective-permute-start.8
  24.7 4.3 %collective-permute-start.3 = (bf16[512,128]{1,0:T(8,128)(2,1)S(1)}, bf16[512,128]{1,0:T(8,128)(2,1)S(1)}, u32[]{:S(2)}, u32[]{:S(2)}) collective-permute-start(bf16[512,128]{1,0:T(8,128)(2,1)S(1)} %get-tuple-element.39), channel_id=1, source_target_pairs={{0,4},{1,5},{2,6},{3,7},{4,8},{5,9},{6,10},{7,11},{8,12},{9,13},{1... | collective-permute-start | bytes 393224 | tf_op jit(solution)/shard_map/ppermute | solution.py:26
  29.0 1.3 %collective-permute-start.4 = (bf16[2,512,128]{2,1,0:T(8,128)(2,1)S(1)}, bf16[2,512,128]{2,1,0:T(8,128)(2,1)S(1)}, u32[]{:S(2)}, u32[]{:S(2)}) collective-permute-start(bf16[2,512,128]{2,1,0:T(8,128)(2,1)S(1)} %get-tuple-element.40), channel_id=1, source_target_pairs={{8,0},{9,1},{10,2},{11,3},{12,4},{13,5},{14,6},{15,7},{16,8},{17,9... | collective-permute-start | bytes 786440 | tf_op jit(solution)/shard_map/ppermute | solution.py:26
  30.3 0.0 collective-permute-done.11.w2_ref
  30.3 1.3 %collective-permute-start.6 = (bf16[2,512,128]{2,1,0:T(8,128)(2,1)S(1)}, bf16[2,512,128]{2,1,0:T(8,128)(2,1)S(1)}, u32[]{:S(2)}, u32[]{:S(2)}) collective-permute-start(bf16[2,512,128]{2,1,0:T(8,128)(2,1)S(1)} %get-tuple-element.42), channel_id=1, source_target_pairs={{8,2},{9,3},{10,0},{11,1},{12,6},{13,7},{14,4},{15,5},{16,10},{17,... | collective-permute-start | bytes 786440 | tf_op jit(solution)/shard_map/ppermute | solution.py:26
  31.6 0.8 %collective-permute-done.3.dq_same = bf16[512,128]{1,0:T(8,128)(2,1)S(1)} collective-permute-done((bf16[512,128]{1,0:T(8,128)(2,1)S(1)}, bf16[512,128]{1,0:T(8,128)(2,1)S(1)}, u32[]{:S(2)}, u32[]{:S(2)}) %collective-permute-start.3) | collective-permute-done | bytes 131104 | tf_op jit(solution)/shard_map/ppermute | solution.py:26
  32.4 5.3 %collective-permute-start.5 = (bf16[512,128]{1,0:T(8,128)(2,1)S(1)}, bf16[512,128]{1,0:T(8,128)(2,1)S(1)}, u32[]{:S(2)}, u32[]{:S(2)}) collective-permute-start(bf16[512,128]{1,0:T(8,128)(2,1)S(1)} %get-tuple-element.41), channel_id=1, source_target_pairs={{0,6},{1,7},{2,4},{3,5},{4,10},{5,11},{6,8},{7,9},{8,14},{9,15},{1... | collective-permute-start | bytes 393224 | tf_op jit(solution)/shard_map/ppermute | solution.py:26
  37.7 8.1 %collective-permute-done.5.dq_cross = bf16[512,128]{1,0:T(8,128)(2,1)S(1)} collective-permute-done((bf16[512,128]{1,0:T(8,128)(2,1)S(1)}, bf16[512,128]{1,0:T(8,128)(2,1)S(1)}, u32[]{:S(2)}, u32[]{:S(2)}) %collective-permute-start.5) | collective-permute-done | bytes 131104 | tf_op jit(solution)/shard_map/ppermute | solution.py:26
  45.9 0.0 collective-permute-start.12
  45.9 0.0 collective-permute-done.4.dkv_same
  45.9 0.1 collective-permute-done.6.dkv_cross
  46.0 0.1 shard_map.69
  46.0 0.5 collective-permute-start.7
  46.5 0.0 collective-permute-done.9.w1_ref
  46.5 0.0 collective-permute-done.8.got_ref
  46.5 0.6 %shard_map.70 = (f32[256,512]{1,0:T(8,128)S(1)}, bf16[256,512]{1,0:T(8,128)(2,1)S(1)}) custom-call(bf16[3,512,128]{2,1,0:T(8,128)(2,1)S(1)} %get-tuple-element.45.keep_ref, bf16[3,512,128]{2,1,0:T(8,128)(2,1)S(1)} %collective-permute-done.8.got_ref, bf16[3,512,128]{2,1,0:T(8,128)(2,1)S(1)} %copy-done, bf16[3,512,128]{2,1,0:T(8,128)(2,1)S(1)} %collective-permute-done.9.w1_ref), custom_call_target="tpu_custom_call" | custom-call | flops 201326592 | bytes 2359296 | tf_op jit(solution)/shard_map/pallas_call | solution.py:267
  47.1 0.6 %collective-permute-start.10 = (bf16[256,512]{1,0:T(8,128)(2,1)S(1)}, bf16[256,512]{1,0:T(8,128)(2,1)S(1)}, u32[]{:S(2)}, u32[]{:S(2)}) collective-permute-start(bf16[256,512]{1,0:T(8,128)(2,1)S(1)} %get-tuple-element.48), channel_id=1, source_target_pairs={{0,2},{1,3},{2,0},{3,1},{4,6},{5,7},{6,4},{7,5},{8,10},{9,11},{10,... | collective-permute-start | bytes 786440 | tf_op jit(solution)/shard_map/ppermute | solution.py:26
  47.7 0.0 collective-permute-done.12.w3_ref
  47.7 0.4 collective-permute-done.7.got_ref
  48.1 7.4 %collective-permute-done.10.arrived_ref = bf16[256,512]{1,0:T(8,128)(2,1)S(1)} collective-permute-done((bf16[256,512]{1,0:T(8,128)(2,1)S(1)}, bf16[256,512]{1,0:T(8,128)(2,1)S(1)}, u32[]{:S(2)}, u32[]{:S(2)}) %collective-permute-start.10) | collective-permute-done | bytes 262176 | tf_op jit(solution)/shard_map/ppermute | solution.py:26
  55.5 1.4 %shard_map.71 = f32[256,512]{1,0:T(8,128)} custom-call(bf16[2,3,256,128]{3,2,1,0:T(8,128)(2,1)S(1)} %get-tuple-element.43.keep_ref, bf16[2,3,256,128]{3,2,1,0:T(8,128)(2,1)S(1)} %collective-permute-done.7.got_ref, f32[256,512]{1,0:T(8,128)S(1)} %get-tuple-element.47.mine_ref, bf16[256,512]{1,0:T(8,128)(2,1)S(1)} %collective-permute-done.10.arrived_ref, ...), custom_call_target="tpu_custom_call" | custom-call | flops 402653184 | bytes 3670016 | tf_op jit(solution)/shard_map/pallas_call | solution.py:267
Async XLA Ops:
  0.0 7.6 %copy-start = (bf16[3,512,128]{2,1,0:T(8,128)(2,1)S(1)}, bf16[3,512,128]{2,1,0:T(8,128)(2,1)}, u32[]{:S(2)}) copy-start(bf16[3,512,128]{2,1,0:T(8,128)(2,1)} %w_ref.3) | copy-start | bytes 1179652
  1.3 18.5 %collective-permute-start.2 = (bf16[2,1024,128]{2,1,0:T(8,128)(2,1)S(1)}, bf16[2,1024,128]{2,1,0:T(8,128)(2,1)S(1)}, u32[]{:S(2)}, u32[]{:S(2)}) collective-permute-start(bf16[2,1024,128]{2,1,0:T(8,128)(2,1)S(1)} %get-tuple-element.29.kv_ref), channel_id=1, source_target_pairs={{0,8},{1,9},{2,10},{3,11},{4,12},{5,13},{6,14},{7,15},{8,16},{9,17... | collective-permute-start | bytes 1572872 | tf_op jit(solution)/shard_map/ppermute | solution.py:26
  6.3 4.2 %copy-start.1 = (s32[4]{0:T(128)S(1)}, s32[4]{0:T(128)}, u32[]{:S(2)}) copy-start(s32[4]{0:T(128)} %lengths_ref.7) | copy-start | bytes 52
  6.3 10.8 %collective-permute-start = (bf16[2,512,128]{2,1,0:T(8,128)(2,1)S(1)}, bf16[2,512,128]{2,1,0:T(8,128)(2,1)S(1)}, u32[]{:S(2)}, u32[]{:S(2)}) collective-permute-start(bf16[2,512,128]{2,1,0:T(8,128)(2,1)S(1)} %get-tuple-element.27.qa_ref), channel_id=1, source_target_pairs={{4,0},{5,1},{6,2},{7,3},{8,4},{9,5},{10,6},{11,7},{12,8},{13,9},{1... | collective-permute-start | bytes 786440 | tf_op jit(solution)/shard_map/ppermute | solution.py:26
  7.6 38.9 %collective-permute-start.9 = (bf16[3,512,128]{2,1,0:T(8,128)(2,1)S(1)}, bf16[3,512,128]{2,1,0:T(8,128)(2,1)S(1)}, u32[]{:S(2)}, u32[]{:S(2)}) collective-permute-start(bf16[3,512,128]{2,1,0:T(8,128)(2,1)S(1)} %copy-done), channel_id=1, source_target_pairs={{0,1},{1,0},{2,3},{3,2},{4,5},{5,4},{6,7},{7,6},{8,9},{9,8},{10,11... | collective-permute-start | bytes 1179656 | tf_op jit(solution)/shard_map/ppermute | solution.py:26
  7.7 22.6 %collective-permute-start.11 = (bf16[3,512,128]{2,1,0:T(8,128)(2,1)S(1)}, bf16[3,512,128]{2,1,0:T(8,128)(2,1)S(1)}, u32[]{:S(2)}, u32[]{:S(2)}) collective-permute-start(bf16[3,512,128]{2,1,0:T(8,128)(2,1)S(1)} %copy-done), channel_id=1, source_target_pairs={{0,2},{1,3},{2,0},{3,1},{4,6},{5,7},{6,4},{7,5},{8,10},{9,11},{10,... | collective-permute-start | bytes 1179656 | tf_op jit(solution)/shard_map/ppermute | solution.py:26
  9.2 12.3 %collective-permute-start.1 = (bf16[2,512,128]{2,1,0:T(8,128)(2,1)S(1)}, bf16[2,512,128]{2,1,0:T(8,128)(2,1)S(1)}, u32[]{:S(2)}, u32[]{:S(2)}) collective-permute-start(bf16[2,512,128]{2,1,0:T(8,128)(2,1)S(1)} %get-tuple-element.28.qb_ref), channel_id=1, source_target_pairs={{4,0},{5,1},{6,2},{7,3},{8,4},{9,5},{10,6},{11,7},{12,8},{13,9},{1... | collective-permute-start | bytes 786440 | tf_op jit(solution)/shard_map/ppermute | solution.py:26
  24.6 21.9 %collective-permute-start.8 = (bf16[3,512,128]{2,1,0:T(8,128)(2,1)S(1)}, bf16[3,512,128]{2,1,0:T(8,128)(2,1)S(1)}, u32[]{:S(2)}, u32[]{:S(2)}) collective-permute-start(bf16[3,512,128]{2,1,0:T(8,128)(2,1)S(1)} %get-tuple-element.46), channel_id=1, source_target_pairs={{0,1},{1,0},{2,3},{3,2},{4,5},{5,4},{6,7},{7,6},{8,9},{9,8},{10,11... | collective-permute-start | bytes 1179656 | tf_op jit(solution)/shard_map/ppermute | solution.py:26
  24.7 7.7 %collective-permute-start.3 = (bf16[512,128]{1,0:T(8,128)(2,1)S(1)}, bf16[512,128]{1,0:T(8,128)(2,1)S(1)}, u32[]{:S(2)}, u32[]{:S(2)}) collective-permute-start(bf16[512,128]{1,0:T(8,128)(2,1)S(1)} %get-tuple-element.39), channel_id=1, source_target_pairs={{0,4},{1,5},{2,6},{3,7},{4,8},{5,9},{6,10},{7,11},{8,12},{9,13},{1... | collective-permute-start | bytes 393224 | tf_op jit(solution)/shard_map/ppermute | solution.py:26
  29.0 16.8 %collective-permute-start.4 = (bf16[2,512,128]{2,1,0:T(8,128)(2,1)S(1)}, bf16[2,512,128]{2,1,0:T(8,128)(2,1)S(1)}, u32[]{:S(2)}, u32[]{:S(2)}) collective-permute-start(bf16[2,512,128]{2,1,0:T(8,128)(2,1)S(1)} %get-tuple-element.40), channel_id=1, source_target_pairs={{8,0},{9,1},{10,2},{11,3},{12,4},{13,5},{14,6},{15,7},{16,8},{17,9... | collective-permute-start | bytes 786440 | tf_op jit(solution)/shard_map/ppermute | solution.py:26
  30.3 15.6 %collective-permute-start.6 = (bf16[2,512,128]{2,1,0:T(8,128)(2,1)S(1)}, bf16[2,512,128]{2,1,0:T(8,128)(2,1)S(1)}, u32[]{:S(2)}, u32[]{:S(2)}) collective-permute-start(bf16[2,512,128]{2,1,0:T(8,128)(2,1)S(1)} %get-tuple-element.42), channel_id=1, source_target_pairs={{8,2},{9,3},{10,0},{11,1},{12,6},{13,7},{14,4},{15,5},{16,10},{17,... | collective-permute-start | bytes 786440 | tf_op jit(solution)/shard_map/ppermute | solution.py:26
  32.4 13.5 %collective-permute-start.5 = (bf16[512,128]{1,0:T(8,128)(2,1)S(1)}, bf16[512,128]{1,0:T(8,128)(2,1)S(1)}, u32[]{:S(2)}, u32[]{:S(2)}) collective-permute-start(bf16[512,128]{1,0:T(8,128)(2,1)S(1)} %get-tuple-element.41), channel_id=1, source_target_pairs={{0,6},{1,7},{2,4},{3,5},{4,10},{5,11},{6,8},{7,9},{8,14},{9,15},{1... | collective-permute-start | bytes 393224 | tf_op jit(solution)/shard_map/ppermute | solution.py:26
  45.9 1.9 %collective-permute-start.12 = (bf16[3,512,128]{2,1,0:T(8,128)(2,1)S(1)}, bf16[3,512,128]{2,1,0:T(8,128)(2,1)S(1)}, u32[]{:S(2)}, u32[]{:S(2)}) collective-permute-start(bf16[3,512,128]{2,1,0:T(8,128)(2,1)S(1)} %collective-permute-done.11.w2_ref), channel_id=1, source_target_pairs={{0,1},{1,0},{2,3},{3,2},{4,5},{5,4},{6,7},{7,6},{8,9},{9,8},{10,11... | collective-permute-start | bytes 1179656 | tf_op jit(solution)/shard_map/ppermute | solution.py:26
  46.0 2.1 %collective-permute-start.7 = (bf16[2,3,256,128]{3,2,1,0:T(8,128)(2,1)S(1)}, bf16[2,3,256,128]{3,2,1,0:T(8,128)(2,1)S(1)}, u32[]{:S(2)}, u32[]{:S(2)}) collective-permute-start(bf16[2,3,256,128]{3,2,1,0:T(8,128)(2,1)S(1)} %get-tuple-element.44), channel_id=1, source_target_pairs={{0,1},{1,0},{2,3},{3,2},{4,5},{5,4},{6,7},{7,6},{8,9},{9,8},{10,11... | collective-permute-start | bytes 1179656 | tf_op jit(solution)/shard_map/ppermute | solution.py:26
  47.1 8.4 %collective-permute-start.10 = (bf16[256,512]{1,0:T(8,128)(2,1)S(1)}, bf16[256,512]{1,0:T(8,128)(2,1)S(1)}, u32[]{:S(2)}, u32[]{:S(2)}) collective-permute-start(bf16[256,512]{1,0:T(8,128)(2,1)S(1)} %get-tuple-element.48), channel_id=1, source_target_pairs={{0,2},{1,3},{2,0},{3,1},{4,6},{5,7},{6,4},{7,5},{8,10},{9,11},{10,... | collective-permute-start | bytes 786440 | tf_op jit(solution)/shard_map/ppermute | solution.py:26
where the time goes:
time: 57.9 us; the launch traced here: 56.9 us
  starting transfers between devices  22.5 us (39%)
  waiting for transfers between devices  20.7 us (36%)
  Pallas kernels  13.5 us (23%)
    ppermute x13, starting transfers between devices, shift(): return lax.ppermute(value, ('seq', 'head'), pairs)  22.5 us
    ppermute x13, waiting for transfers between devices, shift(): return lax.ppermute(value, ('seq', 'head'), pairs)  20.7 us
    pallas_call x8, Pallas kernels, call(): pl.pallas_call(body, out_shape=outs, in_specs=specs, out_specs=tuple((VME...  13.5 us
  transfers between devices with their start and end apart: 13, of which 7 were waited for; matrix products, arithmetic and copies ran while one was open for 0% of the time, Pallas kernels for 19%

commit v1 on v0

--- a/solution.py
+++ b/solution.py
@@ -188,7 +188,7 @@
 def rest_kernel(
     lengths_ref, qan_ref, qbn_ref, kv_ref, kvn_ref,
     dq_ref, dqa_in, dk_in, dv_in, dkn_in, dvn_in,
-    keep_ref, send_ref, dq_same, dq_cross, dkv_same, dkv_cross,
+    dqn_out, dkv_same, dkv_cross,
     dqa_ref, dk_own, dv_own, dk_ref, dv_ref,
     dqb_ref, *masked,
 ):
@@ -206,21 +206,28 @@
 
     norm = MAXLEN**-0.5
     inner = 0.5 * norm * width**-0.5
-    half = dq_same.shape[0]
-    block = half // 2
-    head = lax.axis_index("head")
-    high, low = head // 2, head % 2
-    for bit, dq_out, dkv_out in ((high, dq_same, dkv_same), (1 - high, dq_cross, dkv_cross)):
+    half = rows // 2
+    dqn_out[pl.ds(0, half), :] = (dqa_ref[...] * inner).astype(BF16)
+    dqn_out[pl.ds(half, half), :] = (dqb_ref[...] * inner).astype(BF16)
+    high = lax.axis_index("head") // 2
+    for bit, dkv_out in ((high, dkv_same), (1 - high, dkv_cross)):
         src = pl.ds(pl.multiple_of(bit * half, half), half)
-        dq_out[...] = (jnp.where(bit == 0, dqa_ref[...], dqb_ref[...]) * inner).astype(BF16)
         dkv_out[0] = (dk_ref[src, :] * inner).astype(BF16)
         dkv_out[1] = (dv_ref[src, :] * norm).astype(BF16)
-    for bit, out_ref in ((low, keep_ref), (1 - low, send_ref)):
+
+
+def join_kernel(dq_ref, dk_ref, dv_ref, dq_got, keep_ref, send_ref):
+    width = dq_ref.shape[1]
+    block = keep_ref.shape[1] // 2
+    norm = MAXLEN**-0.5
+    inner = 0.5 * norm * width**-0.5
+    low = lax.axis_index("head") % 2
+    for bit, out_ref in ((1 - low, send_ref), (low, keep_ref)):
         for top in range(2):
             src = pl.ds(pl.multiple_of((2 * top + bit) * block, block), block)
             dst = pl.ds(top * block, block)
-            own = (dq_ref[src, :] * inner, dk_own[src, :] * inner, dv_own[src, :] * norm)
-            for c, part in enumerate(own):
+            dq = dq_ref[src, :] * inner + dq_got[src, :].astype(F32)
+            for c, part in enumerate((dq, dk_ref[src, :] * inner, dv_ref[src, :] * norm)):
                 out_ref[c, dst, :] = part.astype(BF16)
 
 
@@ -241,24 +248,29 @@
         out_ref[...] = project(grads, weights).astype(out_ref.dtype)
 
 
-def split_kernel(dq_same, dkv_same, dq_cross, dkv_cross, keep_ref, send_ref):
+def split_kernel(dkv_same, dkv_cross, keep_ref, send_ref):
     block = keep_ref.shape[2]
     low = lax.axis_index("head") % 2
     for bit, out_ref in ((1 - low, send_ref), (low, keep_ref)):
         src = pl.ds(pl.multiple_of(bit * block, block), block)
-        for n, (dq, dkv) in enumerate(((dq_same, dkv_same), (dq_cross, dkv_cross))):
-            out_ref[n, 0] = dq[src, :]
-            out_ref[n, 1] = dkv[0, src, :]
-            out_ref[n, 2] = dkv[1, src, :]
-
-
-def final_kernel(keep_ref, got_ref, mine_ref, arrived_ref, w_ref, w1_ref, w2_ref, w3_ref, out_ref):
-    grads, weights = [], []
-    for half_ref, pair in ((keep_ref, (w_ref, w2_ref)), (got_ref, (w1_ref, w3_ref))):
-        for n, weight in enumerate(pair):
-            grads += [half_ref[n, c] for c in range(3)]
-            weights += [weight[c] for c in range(3)]
-    out_ref[...] = project(grads, weights) + mine_ref[...] + arrived_ref[...].astype(F32)
+        for n, dkv in enumerate((dkv_same, dkv_cross)):
+            for c in range(2):
+                out_ref[n, c] = dkv[c, src, :]
+
+
+def returned(half_ref, weights):
+    grads = [half_ref[n, c] for n in range(2) for c in range(2)]
+    return project(grads, [weight[c] for weight in weights for c in (1, 2)])
+
+
+def partial_kernel(keep_ref, mine_ref, w_ref, w2_ref, out_ref):
+    out_ref[...] = mine_ref[...] + returned(keep_ref, (w_ref, w2_ref))
+
+
+def final_kernel(got_ref, partial_ref, arrived_ref, w1_ref, w3_ref, out_ref):
+    out_ref[...] = (
+        partial_ref[...] + arrived_ref[...].astype(F32) + returned(got_ref, (w1_ref, w3_ref))
+    )
 
 
 def call(body, outs, args, flops, scratch=(), lengths=True, space=VMEM, aliases=()):
@@ -311,23 +323,24 @@
         near_kernel, (wide, wide, wide), (lengths, qa, qb, kvn, dq), pair_flops,
         scratch=masked, aliases=((4, 0),),
     )
-    keep, send, dq_same, dq_cross, dkv_same, dkv_cross, *_ = call(
+    dqn, dkv_same, dkv_cross, _, dk, dv, *_ = call(
         rest_kernel,
         (
-            like((3, 2 * block, width), BF16), like((3, 2 * block, width), BF16),
-            like((2 * block, width), BF16), like((2 * block, width), BF16),
+            like((rows, width), BF16),
             like((2, 2 * block, width), BF16), like((2, 2 * block, width), BF16),
             half_wide, wide, wide, wide, wide,
         ),
         (lengths, qan, qbn, kv, kvn, dq, dqn, dk, dv, dkn, dvn), pair_flops,
         scratch=[pltpu.VMEM((rows // 2, width), F32), *masked],
-        aliases=((6, 6), (7, 7), (8, 8), (9, 9), (10, 10)),
+        aliases=((6, 3), (7, 4), (8, 5), (9, 6), (10, 7)),
     )
     w1, w3 = shift(w_proj, 0, 1), shift(w2, 0, 1)
+    dq_got = shift(dqn, 1)
     dkv_cross = shift(dkv_cross, -2, 2)
     dkv_same = shift(dkv_same, -2)
-    dq_cross = shift(dq_cross, 1, 2)
-    dq_same = shift(dq_same, 1)
+
+    packed = like((3, 2 * block, width), BF16)
+    keep, send = call(join_kernel, (packed, packed), (dq, dk, dv, dq_got), 1000, lengths=False)
     got = shift(send, 0, 1)
     mine, send = call(
         local_kernel, (like((block, model), F32), like((block, model), BF16)),
@@ -335,15 +348,16 @@
     )
     arrived = shift(send, 0, 2)
 
-    quarter = like((2, 3, block, width), BF16)
-    keep, send = call(
-        split_kernel, (quarter, quarter), (dq_same, dkv_same, dq_cross, dkv_cross), 1000,
-        lengths=False,
-    )
+    quarter = like((2, 2, block, width), BF16)
+    keep, send = call(split_kernel, (quarter, quarter), (dkv_same, dkv_cross), 1000, lengths=False)
     got = shift(send, 0, 1)
+    (mine,) = call(
+        partial_kernel, (like((block, model), F32),), (keep, mine, w_proj, w2),
+        8 * block * width * model, lengths=False,
+    )
     (out,) = call(
-        final_kernel, (like((block, model), F32),),
-        (keep, got, mine, arrived, w_proj, w1, w2, w3), 24 * block * width * model, lengths=False,
+        final_kernel, (like((block, model), F32),), (got, mine, arrived, w1, w3),
+        8 * block * width * model, lengths=False,
     )
     return out
 

time: 57.9 us -> 62.1 us (1.073); the launches traced: 56.9 us -> 61.8 us
  waiting for transfers between devices: 20.7 us -> 31.3 us
  starting transfers between devices: 22.5 us -> 16.8 us
    ppermute x13 -> x12, waiting for transfers between devices: 20.7 us -> 31.3 us  [shift(): return lax.ppermute(value, ('seq', 'head'), pairs)]
    ppermute x13 -> x12, starting transfers between devices: 22.5 us -> 16.8 us  [shift(): return lax.ppermute(value, ('seq', 'head'), pairs)]
    pallas_call x8 -> x10, Pallas kernels: 13.5 us -> 13.5 us  [call(): pl.pallas_call(body, out_shape=outs, in_specs=specs, out_specs=tuple((VME...]
  transfers between devices with their start and end apart: 13 -> 12, of which waited for: 7 -> 7; matrix products, arithmetic and copies ran while one was open for 0% -> 0% of each run, Pallas kernels for 19% -> 13%
where the time goes in v1:
time: 62.1 us; the launch traced here: 61.8 us
  waiting for transfers between devices  31.3 us (50%)
  starting transfers between devices  16.8 us (27%)
  Pallas kernels  13.5 us (22%)
    ppermute x12, waiting for transfers between devices, shift(): return lax.ppermute(value, ('seq', 'head'), pairs)  31.3 us
    ppermute x12, starting transfers between devices, shift(): return lax.ppermute(value, ('seq', 'head'), pairs)  16.8 us
    pallas_call x10, Pallas kernels, call(): pl.pallas_call(body, out_shape=outs, in_specs=specs, out_specs=tuple((VME...  13.5 us
  transfers between devices with their start and end apart: 12, of which 7 were waited for; matrix products, arithmetic and copies ran while one was open for 0% of the time, Pallas kernels for 13%

profile of v1, /device:TPU:0, one launch (start us, length us, event | category | flops | bytes accessed | tf_op | source)
XLA Modules:
  0.0 61.8 jit_solution(7838746428909458643)
XLA Ops:
  0.0 1.2 %shard_map.64 = (bf16[2,512,128]{2,1,0:T(8,128)(2,1)S(1)}, bf16[2,512,128]{2,1,0:T(8,128)(2,1)S(1)}, bf16[2,1024,128]{2,1,0:T(8,128)(2,1)S(1)}) custom-call(bf16[1024,128]{1,0:T(8,128)(2,1)} %q_hbm.1, bf16[1024,128]{1,0:T(8,128)(2,1)} %g_hbm.1, bf16[1024,128]{1,0:T(8,128)(2,1)} %k_hbm.1, bf16[1024,128]{1,0:T(8,128)(2,1)} %v_hbm.1), custom_call_target="tpu_custom_call" | custom-call | flops 1000 | bytes 2097152 | tf_op jit(solution)/shard_map/pallas_call | solution.py:279
  1.2 5.0 %collective-permute-start.2 = (bf16[2,1024,128]{2,1,0:T(8,128)(2,1)S(1)}, bf16[2,1024,128]{2,1,0:T(8,128)(2,1)S(1)}, u32[]{:S(2)}, u32[]{:S(2)}) collective-permute-start(bf16[2,1024,128]{2,1,0:T(8,128)(2,1)S(1)} %get-tuple-element.30.kv_ref), channel_id=1, source_target_pairs={{0,8},{1,9},{2,10},{3,11},{4,12},{5,13},{6,14},{7,15},{8,16},{9,17... | collective-permute-start | bytes 1572872 | tf_op jit(solution)/shard_map/ppermute | solution.py:26
  6.2 0.0 copy-start.1
  6.2 1.3 %collective-permute-start = (bf16[2,512,128]{2,1,0:T(8,128)(2,1)S(1)}, bf16[2,512,128]{2,1,0:T(8,128)(2,1)S(1)}, u32[]{:S(2)}, u32[]{:S(2)}) collective-permute-start(bf16[2,512,128]{2,1,0:T(8,128)(2,1)S(1)} %get-tuple-element.28.qa_ref), channel_id=1, source_target_pairs={{4,0},{5,1},{6,2},{7,3},{8,4},{9,5},{10,6},{11,7},{12,8},{13,9},{1... | collective-permute-start | bytes 786440 | tf_op jit(solution)/shard_map/ppermute | solution.py:26
  7.5 1.3 %collective-permute-start.1 = (bf16[2,512,128]{2,1,0:T(8,128)(2,1)S(1)}, bf16[2,512,128]{2,1,0:T(8,128)(2,1)S(1)}, u32[]{:S(2)}, u32[]{:S(2)}) collective-permute-start(bf16[2,512,128]{2,1,0:T(8,128)(2,1)S(1)} %get-tuple-element.29.qb_ref), channel_id=1, source_target_pairs={{4,0},{5,1},{6,2},{7,3},{8,4},{9,5},{10,6},{11,7},{12,8},{13,9},{1... | collective-permute-start | bytes 786440 | tf_op jit(solution)/shard_map/ppermute | solution.py:26
  8.8 0.0 copy-done.1
  8.9 3.8 %shard_map.65 = (f32[1024,128]{1,0:T(8,128)S(1)}, f32[1024,128]{1,0:T(8,128)S(1)}, f32[1024,128]{1,0:T(8,128)S(1)}) custom-call(s32[4]{0:T(128)S(1)} %copy-done.1, bf16[2,512,128]{2,1,0:T(8,128)(2,1)S(1)} %get-tuple-element.28.qa_ref, bf16[2,512,128]{2,1,0:T(8,128)(2,1)S(1)} %get-tuple-element.29.qb_ref, bf16[2,1024,128]{2,1,0:T(8,128)(2,1)S(1)} %get-tuple-element.30.kv_ref), custom_call_target="tpu_custom_call" | custom-call | flops 1342177280 | bytes 2621456 | tf_op jit(solution)/shard_map/pallas_call | solution.py:279
  12.6 4.7 %collective-permute-done.qan_ref = bf16[2,512,128]{2,1,0:T(8,128)(2,1)S(1)} collective-permute-done((bf16[2,512,128]{2,1,0:T(8,128)(2,1)S(1)}, bf16[2,512,128]{2,1,0:T(8,128)(2,1)S(1)}, u32[]{:S(2)}, u32[]{:S(2)}) %collective-permute-start) | collective-permute-done | bytes 262176 | tf_op jit(solution)/shard_map/ppermute | solution.py:26
  17.3 2.7 %shard_map.67 = (f32[512,128]{1,0:T(8,128)S(1)}, f32[1024,128]{1,0:T(8,128)S(1)}, f32[1024,128]{1,0:T(8,128)S(1)}) custom-call(s32[4]{0:T(128)S(1)} %copy-done.1, bf16[2,512,128]{2,1,0:T(8,128)(2,1)S(1)} %collective-permute-done.qan_ref, bf16[2,1024,128]{2,1,0:T(8,128)(2,1)S(1)} %get-tuple-element.30.kv_ref, ...), custom_call_target="tpu_custom_call", output_to_operand_aliasing={{1}: (3, {}), {2}: (4, {})} | custom-call | flops 1342177280 | bytes 3145744 | tf_op jit(solution)/shard_map/pallas_call | solution.py:279
  20.0 0.0 collective-permute-done.2.kvn_ref
  20.0 0.7 %shard_map.66 = (f32[1024,128]{1,0:T(8,128)S(1)}, f32[1024,128]{1,0:T(8,128)S(1)}, f32[1024,128]{1,0:T(8,128)S(1)}) custom-call(s32[4]{0:T(128)S(1)} %copy-done.1, bf16[2,512,128]{2,1,0:T(8,128)(2,1)S(1)} %get-tuple-element.28.qa_ref, bf16[2,512,128]{2,1,0:T(8,128)(2,1)S(1)} %get-tuple-element.29.qb_ref, ...), custom_call_target="tpu_custom_call", output_to_operand_aliasing={{0}: (4, {})} | custom-call | flops 1342177280 | bytes 3145744 | tf_op jit(solution)/shard_map/pallas_call | solution.py:279
  20.7 0.8 %collective-permute-done.1.qbn_ref = bf16[2,512,128]{2,1,0:T(8,128)(2,1)S(1)} collective-permute-done((bf16[2,512,128]{2,1,0:T(8,128)(2,1)S(1)}, bf16[2,512,128]{2,1,0:T(8,128)(2,1)S(1)}, u32[]{:S(2)}, u32[]{:S(2)}) %collective-permute-start.1) | collective-permute-done | bytes 262176 | tf_op jit(solution)/shard_map/ppermute | solution.py:26
  21.5 0.0 copy-start
  21.5 2.9 %shard_map.68 = (bf16[1024,128]{1,0:T(8,128)(2,1)S(1)}, bf16[2,512,128]{2,1,0:T(8,128)(2,1)S(1)}, bf16[2,512,128]{2,1,0:T(8,128)(2,1)S(1)}, f32[512,128]{1,0:T(8...) custom-call(s32[4]{0:T(128)S(1)} %copy-done.1, ...), custom_call_target="tpu_custom_call", output_to_operand_aliasing={{3}: (6, {}), {4}: (7, {}), {5}: (8, {}), {6}: (9, {}), {7}... | custom-call | flops 1342177280 | bytes 7602192 | tf_op jit(solution)/shard_map/pallas_call | solution.py:279
  24.4 4.3 %collective-permute-start.6 = (bf16[1024,128]{1,0:T(8,128)(2,1)S(1)}, bf16[1024,128]{1,0:T(8,128)(2,1)S(1)}, u32[]{:S(2)}, u32[]{:S(2)}) collective-permute-start(bf16[1024,128]{1,0:T(8,128)(2,1)S(1)} %get-tuple-element.46), channel_id=1, source_target_pairs={{0,4},{1,5},{2,6},{3,7},{4,8},{5,9},{6,10},{7,11},{8,12},{9,13},{1... | collective-permute-start | bytes 786440 | tf_op jit(solution)/shard_map/ppermute | solution.py:26
  28.8 0.0 copy-done
  28.8 1.6 %collective-permute-start.9 = (bf16[3,512,128]{2,1,0:T(8,128)(2,1)S(1)}, bf16[3,512,128]{2,1,0:T(8,128)(2,1)S(1)}, u32[]{:S(2)}, u32[]{:S(2)}) collective-permute-start(bf16[3,512,128]{2,1,0:T(8,128)(2,1)S(1)} %copy-done), channel_id=1, source_target_pairs={{0,2},{1,3},{2,0},{3,1},{4,6},{5,7},{6,4},{7,5},{8,10},{9,11},{10,... | collective-permute-start | bytes 1179656 | tf_op jit(solution)/shard_map/ppermute | solution.py:26
  30.3 0.0 collective-permute-start.8
  30.3 2.8 %collective-permute-done.6.dq_got = bf16[1024,128]{1,0:T(8,128)(2,1)S(1)} collective-permute-done((bf16[1024,128]{1,0:T(8,128)(2,1)S(1)}, bf16[1024,128]{1,0:T(8,128)(2,1)S(1)}, u32[]{:S(2)}, u32[]{:S(2)}) %collective-permute-start.6) | collective-permute-done | bytes 262176 | tf_op jit(solution)/shard_map/ppermute | solution.py:26
  33.2 0.1 shard_map.70
  33.3 0.1 collective-permute-start.7
  33.4 1.3 %collective-permute-start.3 = (bf16[2,512,128]{2,1,0:T(8,128)(2,1)S(1)}, bf16[2,512,128]{2,1,0:T(8,128)(2,1)S(1)}, u32[]{:S(2)}, u32[]{:S(2)}) collective-permute-start(bf16[2,512,128]{2,1,0:T(8,128)(2,1)S(1)} %get-tuple-element.40), channel_id=1, source_target_pairs={{8,0},{9,1},{10,2},{11,3},{12,4},{13,5},{14,6},{15,7},{16,8},{17,9... | collective-permute-start | bytes 786440 | tf_op jit(solution)/shard_map/ppermute | solution.py:26
  34.7 1.3 %collective-permute-start.4 = (bf16[2,512,128]{2,1,0:T(8,128)(2,1)S(1)}, bf16[2,512,128]{2,1,0:T(8,128)(2,1)S(1)}, u32[]{:S(2)}, u32[]{:S(2)}) collective-permute-start(bf16[2,512,128]{2,1,0:T(8,128)(2,1)S(1)} %get-tuple-element.41), channel_id=1, source_target_pairs={{8,2},{9,3},{10,0},{11,1},{12,6},{13,7},{14,4},{15,5},{16,10},{17,... | collective-permute-start | bytes 786440 | tf_op jit(solution)/shard_map/ppermute | solution.py:26
  36.0 2.3 %collective-permute-done.9.w2_ref = bf16[3,512,128]{2,1,0:T(8,128)(2,1)S(1)} collective-permute-done((bf16[3,512,128]{2,1,0:T(8,128)(2,1)S(1)}, bf16[3,512,128]{2,1,0:T(8,128)(2,1)S(1)}, u32[]{:S(2)}, u32[]{:S(2)}) %collective-permute-start.9) | collective-permute-done | bytes 393248 | tf_op jit(solution)/shard_map/ppermute | solution.py:26
  38.3 0.0 collective-permute-start.11
  38.3 6.5 %collective-permute-done.3.dkv_same = bf16[2,512,128]{2,1,0:T(8,128)(2,1)S(1)} collective-permute-done((bf16[2,512,128]{2,1,0:T(8,128)(2,1)S(1)}, bf16[2,512,128]{2,1,0:T(8,128)(2,1)S(1)}, u32[]{:S(2)}, u32[]{:S(2)}) %collective-permute-start.3) | collective-permute-done | bytes 262176 | tf_op jit(solution)/shard_map/ppermute | solution.py:26
  44.8 6.3 %collective-permute-done.4.dkv_cross = bf16[2,512,128]{2,1,0:T(8,128)(2,1)S(1)} collective-permute-done((bf16[2,512,128]{2,1,0:T(8,128)(2,1)S(1)}, bf16[2,512,128]{2,1,0:T(8,128)(2,1)S(1)}, u32[]{:S(2)}, u32[]{:S(2)}) %collective-permute-start.4) | collective-permute-done | bytes 262176 | tf_op jit(solution)/shard_map/ppermute | solution.py:26
  51.2 0.1 collective-permute-start.5
  51.3 0.0 collective-permute-done.8.w1_ref
  51.3 0.0 collective-permute-done.7.got_ref
  51.3 0.6 shard_map.71
  51.9 0.6 collective-permute-start.10
  52.5 0.3 shard_map.72.partial_ref
  52.8 0.0 collective-permute-done.11.w3_ref
  52.9 0.0 collective-permute-done.5.got_ref
  52.9 7.8 %collective-permute-done.10.arrived_ref = bf16[256,512]{1,0:T(8,128)(2,1)S(1)} collective-permute-done((bf16[256,512]{1,0:T(8,128)(2,1)S(1)}, bf16[256,512]{1,0:T(8,128)(2,1)S(1)}, u32[]{:S(2)}, u32[]{:S(2)}) %collective-permute-start.10) | collective-permute-done | bytes 262176 | tf_op jit(solution)/shard_map/ppermute | solution.py:26
  60.7 1.1 %shard_map.73 = f32[256,512]{1,0:T(8,128)} custom-call(bf16[2,2,256,128]{3,2,1,0:T(8,128)(2,1)S(1)} %collective-permute-done.5.got_ref, f32[256,512]{1,0:T(8,128)S(1)} %shard_map.72.partial_ref, bf16[256,512]{1,0:T(8,128)(2,1)S(1)} %collective-permute-done.10.arrived_ref, bf16[3,512,128]{2,1,0:T(8,128)(2,1)S(1)} %collective-permute-done.8.w1_ref, ...), custom_call_target="tpu_custom_call" | custom-call | flops 134217728 | bytes 2359296 | tf_op jit(solution)/shard_map/pallas_call | solution.py:279
  (1 shorter events, 0.0 us)
Async XLA Ops:
  1.2 18.8 %collective-permute-start.2 = (bf16[2,1024,128]{2,1,0:T(8,128)(2,1)S(1)}, bf16[2,1024,128]{2,1,0:T(8,128)(2,1)S(1)}, u32[]{:S(2)}, u32[]{:S(2)}) collective-permute-start(bf16[2,1024,128]{2,1,0:T(8,128)(2,1)S(1)} %get-tuple-element.30.kv_ref), channel_id=1, source_target_pairs={{0,8},{1,9},{2,10},{3,11},{4,12},{5,13},{6,14},{7,15},{8,16},{9,17... | collective-permute-start | bytes 1572872 | tf_op jit(solution)/shard_map/ppermute | solution.py:26
  6.2 2.6 %copy-start.1 = (s32[4]{0:T(128)S(1)}, s32[4]{0:T(128)}, u32[]{:S(2)}) copy-start(s32[4]{0:T(128)} %lengths_ref.7) | copy-start | bytes 52
  6.2 11.1 %collective-permute-start = (bf16[2,512,128]{2,1,0:T(8,128)(2,1)S(1)}, bf16[2,512,128]{2,1,0:T(8,128)(2,1)S(1)}, u32[]{:S(2)}, u32[]{:S(2)}) collective-permute-start(bf16[2,512,128]{2,1,0:T(8,128)(2,1)S(1)} %get-tuple-element.28.qa_ref), channel_id=1, source_target_pairs={{4,0},{5,1},{6,2},{7,3},{8,4},{9,5},{10,6},{11,7},{12,8},{13,9},{1... | collective-permute-start | bytes 786440 | tf_op jit(solution)/shard_map/ppermute | solution.py:26
  7.5 14.0 %collective-permute-start.1 = (bf16[2,512,128]{2,1,0:T(8,128)(2,1)S(1)}, bf16[2,512,128]{2,1,0:T(8,128)(2,1)S(1)}, u32[]{:S(2)}, u32[]{:S(2)}) collective-permute-start(bf16[2,512,128]{2,1,0:T(8,128)(2,1)S(1)} %get-tuple-element.29.qb_ref), channel_id=1, source_target_pairs={{4,0},{5,1},{6,2},{7,3},{8,4},{9,5},{10,6},{11,7},{12,8},{13,9},{1... | collective-permute-start | bytes 786440 | tf_op jit(solution)/shard_map/ppermute | solution.py:26
  21.5 7.2 %copy-start = (bf16[3,512,128]{2,1,0:T(8,128)(2,1)S(1)}, bf16[3,512,128]{2,1,0:T(8,128)(2,1)}, u32[]{:S(2)}) copy-start(bf16[3,512,128]{2,1,0:T(8,128)(2,1)} %w_ref.3) | copy-start | bytes 1179652
  24.4 8.7 %collective-permute-start.6 = (bf16[1024,128]{1,0:T(8,128)(2,1)S(1)}, bf16[1024,128]{1,0:T(8,128)(2,1)S(1)}, u32[]{:S(2)}, u32[]{:S(2)}) collective-permute-start(bf16[1024,128]{1,0:T(8,128)(2,1)S(1)} %get-tuple-element.46), channel_id=1, source_target_pairs={{0,4},{1,5},{2,6},{3,7},{4,8},{5,9},{6,10},{7,11},{8,12},{9,13},{1... | collective-permute-start | bytes 786440 | tf_op jit(solution)/shard_map/ppermute | solution.py:26
  28.8 9.5 %collective-permute-start.9 = (bf16[3,512,128]{2,1,0:T(8,128)(2,1)S(1)}, bf16[3,512,128]{2,1,0:T(8,128)(2,1)S(1)}, u32[]{:S(2)}, u32[]{:S(2)}) collective-permute-start(bf16[3,512,128]{2,1,0:T(8,128)(2,1)S(1)} %copy-done), channel_id=1, source_target_pairs={{0,2},{1,3},{2,0},{3,1},{4,6},{5,7},{6,4},{7,5},{8,10},{9,11},{10,... | collective-permute-start | bytes 1179656 | tf_op jit(solution)/shard_map/ppermute | solution.py:26
  30.3 20.9 %collective-permute-start.8 = (bf16[3,512,128]{2,1,0:T(8,128)(2,1)S(1)}, bf16[3,512,128]{2,1,0:T(8,128)(2,1)S(1)}, u32[]{:S(2)}, u32[]{:S(2)}) collective-permute-start(bf16[3,512,128]{2,1,0:T(8,128)(2,1)S(1)} %copy-done), channel_id=1, source_target_pairs={{0,1},{1,0},{2,3},{3,2},{4,5},{5,4},{6,7},{7,6},{8,9},{9,8},{10,11... | collective-permute-start | bytes 1179656 | tf_op jit(solution)/shard_map/ppermute | solution.py:26
  33.3 18.0 %collective-permute-start.7 = (bf16[3,512,128]{2,1,0:T(8,128)(2,1)S(1)}, bf16[3,512,128]{2,1,0:T(8,128)(2,1)S(1)}, u32[]{:S(2)}, u32[]{:S(2)}) collective-permute-start(bf16[3,512,128]{2,1,0:T(8,128)(2,1)S(1)} %get-tuple-element.48), channel_id=1, source_target_pairs={{0,1},{1,0},{2,3},{3,2},{4,5},{5,4},{6,7},{7,6},{8,9},{9,8},{10,11... | collective-permute-start | bytes 1179656 | tf_op jit(solution)/shard_map/ppermute | solution.py:26
  33.4 11.4 %collective-permute-start.3 = (bf16[2,512,128]{2,1,0:T(8,128)(2,1)S(1)}, bf16[2,512,128]{2,1,0:T(8,128)(2,1)S(1)}, u32[]{:S(2)}, u32[]{:S(2)}) collective-permute-start(bf16[2,512,128]{2,1,0:T(8,128)(2,1)S(1)} %get-tuple-element.40), channel_id=1, source_target_pairs={{8,0},{9,1},{10,2},{11,3},{12,4},{13,5},{14,6},{15,7},{16,8},{17,9... | collective-permute-start | bytes 786440 | tf_op jit(solution)/shard_map/ppermute | solution.py:26
  34.7 16.5 %collective-permute-start.4 = (bf16[2,512,128]{2,1,0:T(8,128)(2,1)S(1)}, bf16[2,512,128]{2,1,0:T(8,128)(2,1)S(1)}, u32[]{:S(2)}, u32[]{:S(2)}) collective-permute-start(bf16[2,512,128]{2,1,0:T(8,128)(2,1)S(1)} %get-tuple-element.41), channel_id=1, source_target_pairs={{8,2},{9,3},{10,0},{11,1},{12,6},{13,7},{14,4},{15,5},{16,10},{17,... | collective-permute-start | bytes 786440 | tf_op jit(solution)/shard_map/ppermute | solution.py:26
  38.3 14.6 %collective-permute-start.11 = (bf16[3,512,128]{2,1,0:T(8,128)(2,1)S(1)}, bf16[3,512,128]{2,1,0:T(8,128)(2,1)S(1)}, u32[]{:S(2)}, u32[]{:S(2)}) collective-permute-start(bf16[3,512,128]{2,1,0:T(8,128)(2,1)S(1)} %collective-permute-done.9.w2_ref), channel_id=1, source_target_pairs={{0,1},{1,0},{2,3},{3,2},{4,5},{5,4},{6,7},{7,6},{8,9},{9,8},{10,11... | collective-permute-start | bytes 1179656 | tf_op jit(solution)/shard_map/ppermute | solution.py:26
  51.2 1.7 %collective-permute-start.5 = (bf16[2,2,256,128]{3,2,1,0:T(8,128)(2,1)S(1)}, bf16[2,2,256,128]{3,2,1,0:T(8,128)(2,1)S(1)}, u32[]{:S(2)}, u32[]{:S(2)}) collective-permute-start(bf16[2,2,256,128]{3,2,1,0:T(8,128)(2,1)S(1)} %get-tuple-element.42), channel_id=1, source_target_pairs={{0,1},{1,0},{2,3},{3,2},{4,5},{5,4},{6,7},{7,6},{8,9},{9,8},{10,11... | collective-permute-start | bytes 786440 | tf_op jit(solution)/shard_map/ppermute | solution.py:26
  51.9 8.8 %collective-permute-start.10 = (bf16[256,512]{1,0:T(8,128)(2,1)S(1)}, bf16[256,512]{1,0:T(8,128)(2,1)S(1)}, u32[]{:S(2)}, u32[]{:S(2)}) collective-permute-start(bf16[256,512]{1,0:T(8,128)(2,1)S(1)} %get-tuple-element.50), channel_id=1, source_target_pairs={{0,2},{1,3},{2,0},{3,1},{4,6},{5,7},{6,4},{7,5},{8,10},{9,11},{10,... | collective-permute-start | bytes 786440 | tf_op jit(solution)/shard_map/ppermute | solution.py:26

commit v2 on v0

--- a/solution.py
+++ b/solution.py
@@ -70,44 +70,61 @@
     dq_ref[qs, :] += lax.dot_general(f, k, (((0,), (0,)), ((), ())), preferred_element_type=F32)
 
 
-def copy_rows(out_ref, ref, start, low, high):
-    block, width = out_ref.shape[1:]
-    src = pl.ds(start, block)
-    inside = (low <= 0) & (high >= block)
+def copy_rows(out_ref, ref, start, count, low, high):
+    src, dst = pl.ds(start, count), pl.ds(0, count)
+    inside = (low <= 0) & (high >= count)
 
     @pl.when(inside)
     def _():
         for n in range(2):
-            out_ref[n] = ref[n, src, :]
+            out_ref[n, dst, :] = ref[n, src, :]
 
     @pl.when(jnp.logical_not(inside))
     def _():
-        row = lax.broadcasted_iota(jnp.int32, (block, width), 0)
+        row = lax.broadcasted_iota(jnp.int32, (count, ref.shape[2]), 0)
         kept = (row >= low) & (row < high)
         for n in range(2):
-            out_ref[n] = jnp.where(kept, ref[n, src, :], jnp.zeros((), BF16))
+            out_ref[n, dst, :] = jnp.where(kept, ref[n, src, :], jnp.zeros((), BF16))
 
 
 def sweep(
     qg_ref, kv_ref, dq_ref, dk_ref, dv_ref, query_rows, key_row, key_blocks, qm_ref, km_ref
 ):
     block = qg_ref.shape[1]
-    everything = pl.ds(0, block)
-
-    @pl.when(query_rows > 0)
+    strip = block // 2
+
+    def run(queries):
+        qs = pl.ds(0, queries)
+        copy_rows(qm_ref, qg_ref, 0, queries, 0, query_rows)
+
+        def keys(start, count):
+            off = pl.multiple_of(start, strip)
+            copy_rows(km_ref, kv_ref, off, count, key_row - off, count)
+            q, g = qm_ref[0, qs, :], qm_ref[1, qs, :]
+            k, v = km_ref[0, pl.ds(0, count), :], km_ref[1, pl.ds(0, count), :]
+            a, f = scores(q, g, k, v)
+            add_block(qs, pl.ds(off, count), q, g, k, a, f, dq_ref, dk_ref, dv_ref)
+
+        first = key_row // block
+        short = key_row - first * block >= strip
+
+        @pl.when(short)
+        def _():
+            keys(first * block + strip, strip)
+
+        def key_block(kb, carry):
+            keys(kb * block, block)
+            return carry
+
+        lax.fori_loop(first + short.astype(jnp.int32), key_blocks, key_block, 0)
+
+    @pl.when((query_rows > 0) & (query_rows <= strip))
     def _():
-        copy_rows(qm_ref, qg_ref, 0, 0, query_rows)
-
-        def key_block(kb, carry):
-            off = pl.multiple_of(kb * block, block)
-            ks = pl.ds(off, block)
-            copy_rows(km_ref, kv_ref, off, key_row - off, block)
-            q, g, k, v = qm_ref[0], qm_ref[1], km_ref[0], km_ref[1]
-            a, f = scores(q, g, k, v)
-            add_block(everything, ks, q, g, k, a, f, dq_ref, dk_ref, dv_ref)
-            return carry
-
-        lax.fori_loop(key_row // block, key_blocks, key_block, 0)
+        run(strip)
+
+    @pl.when(query_rows > strip)
+    def _():
+        run(block)
 
 
 def halves(ref):
@@ -252,13 +269,19 @@
             out_ref[n, 2] = dkv[1, src, :]
 
 
-def final_kernel(keep_ref, got_ref, mine_ref, arrived_ref, w_ref, w1_ref, w2_ref, w3_ref, out_ref):
-    grads, weights = [], []
-    for half_ref, pair in ((keep_ref, (w_ref, w2_ref)), (got_ref, (w1_ref, w3_ref))):
-        for n, weight in enumerate(pair):
-            grads += [half_ref[n, c] for c in range(3)]
-            weights += [weight[c] for c in range(3)]
-    out_ref[...] = project(grads, weights) + mine_ref[...] + arrived_ref[...].astype(F32)
+def returned(half_ref, weights):
+    grads = [half_ref[n, c] for n in range(2) for c in range(3)]
+    return project(grads, [weight[c] for weight in weights for c in range(3)])
+
+
+def partial_kernel(keep_ref, mine_ref, w_ref, w2_ref, out_ref):
+    out_ref[...] = mine_ref[...] + returned(keep_ref, (w_ref, w2_ref))
+
+
+def final_kernel(got_ref, partial_ref, arrived_ref, w1_ref, w3_ref, out_ref):
+    out_ref[...] = (
+        partial_ref[...] + arrived_ref[...].astype(F32) + returned(got_ref, (w1_ref, w3_ref))
+    )
 
 
 def call(body, outs, args, flops, scratch=(), lengths=True, space=VMEM, aliases=()):
@@ -341,9 +364,13 @@
         lengths=False,
     )
     got = shift(send, 0, 1)
+    (mine,) = call(
+        partial_kernel, (like((block, model), F32),), (keep, mine, w_proj, w2),
+        12 * block * width * model, lengths=False,
+    )
     (out,) = call(
-        final_kernel, (like((block, model), F32),),
-        (keep, got, mine, arrived, w_proj, w1, w2, w3), 24 * block * width * model, lengths=False,
+        final_kernel, (like((block, model), F32),), (got, mine, arrived, w1, w3),
+        12 * block * width * model, lengths=False,
     )
     return out
 

time: 57.9 us -> 57.2 us (0.988)
  waiting for transfers between devices: 20.7 us -> 20.1 us
    ppermute x13, waiting for transfers between devices: 20.7 us -> 20.1 us  [shift(): return lax.ppermute(value, ('seq', 'head'), pairs)]
    pallas_call x8 -> x9, Pallas kernels: 13.5 us -> 13.9 us  [call(): pl.pallas_call(body, out_shape=outs, in_specs=specs, out_specs=tuple((VME...]
  transfers between devices with their start and end apart: 13 -> 13, of which waited for: 7 -> 6; matrix products, arithmetic and copies ran while one was open for 0% -> 0% of each run, Pallas kernels for 19% -> 20%
where the time goes in v2:
time: 57.2 us; the launch traced here: 56.7 us
  starting transfers between devices  22.5 us (39%)
  waiting for transfers between devices  20.1 us (35%)
  Pallas kernels  13.9 us (24%)
    ppermute x13, starting transfers between devices, shift(): return lax.ppermute(value, ('seq', 'head'), pairs)  22.5 us
    ppermute x13, waiting for transfers between devices, shift(): return lax.ppermute(value, ('seq', 'head'), pairs)  20.1 us
    pallas_call x9, Pallas kernels, call(): pl.pallas_call(body, out_shape=outs, in_specs=specs, out_specs=tuple((VME...  13.9 us
  transfers between devices with their start and end apart: 13, of which 6 were waited for; matrix products, arithmetic and copies ran while one was open for 0% of the time, Pallas kernels for 20%

profile of v2, /device:TPU:0, one launch (start us, length us, event | category | flops | bytes accessed | tf_op | source)
XLA Modules:
  0.0 56.7 jit_solution(7728709807508561082)
XLA Ops:
  0.0 0.0 copy-start
  0.0 1.3 %shard_map.64 = (bf16[2,512,128]{2,1,0:T(8,128)(2,1)S(1)}, bf16[2,512,128]{2,1,0:T(8,128)(2,1)S(1)}, bf16[2,1024,128]{2,1,0:T(8,128)(2,1)S(1)}) custom-call(bf16[1024,128]{1,0:T(8,128)(2,1)} %q_hbm.1, bf16[1024,128]{1,0:T(8,128)(2,1)} %g_hbm.1, bf16[1024,128]{1,0:T(8,128)(2,1)} %k_hbm.1, bf16[1024,128]{1,0:T(8,128)(2,1)} %v_hbm.1), custom_call_target="tpu_custom_call" | custom-call | flops 1000 | bytes 2097152 | tf_op jit(solution)/shard_map/pallas_call | solution.py:290
  1.3 5.0 %collective-permute-start.2 = (bf16[2,1024,128]{2,1,0:T(8,128)(2,1)S(1)}, bf16[2,1024,128]{2,1,0:T(8,128)(2,1)S(1)}, u32[]{:S(2)}, u32[]{:S(2)}) collective-permute-start(bf16[2,1024,128]{2,1,0:T(8,128)(2,1)S(1)} %get-tuple-element.29.kv_ref), channel_id=1, source_target_pairs={{0,8},{1,9},{2,10},{3,11},{4,12},{5,13},{6,14},{7,15},{8,16},{9,17... | collective-permute-start | bytes 1572872 | tf_op jit(solution)/shard_map/ppermute | solution.py:26
  6.3 0.0 copy-start.1
  6.3 1.3 %collective-permute-start = (bf16[2,512,128]{2,1,0:T(8,128)(2,1)S(1)}, bf16[2,512,128]{2,1,0:T(8,128)(2,1)S(1)}, u32[]{:S(2)}, u32[]{:S(2)}) collective-permute-start(bf16[2,512,128]{2,1,0:T(8,128)(2,1)S(1)} %get-tuple-element.27.qa_ref), channel_id=1, source_target_pairs={{4,0},{5,1},{6,2},{7,3},{8,4},{9,5},{10,6},{11,7},{12,8},{13,9},{1... | collective-permute-start | bytes 786440 | tf_op jit(solution)/shard_map/ppermute | solution.py:26
  7.6 0.0 copy-done
  7.6 0.1 collective-permute-start.9
  7.7 1.6 %collective-permute-start.10 = (bf16[3,512,128]{2,1,0:T(8,128)(2,1)S(1)}, bf16[3,512,128]{2,1,0:T(8,128)(2,1)S(1)}, u32[]{:S(2)}, u32[]{:S(2)}) collective-permute-start(bf16[3,512,128]{2,1,0:T(8,128)(2,1)S(1)} %copy-done), channel_id=1, source_target_pairs={{0,2},{1,3},{2,0},{3,1},{4,6},{5,7},{6,4},{7,5},{8,10},{9,11},{10,... | collective-permute-start | bytes 1179656 | tf_op jit(solution)/shard_map/ppermute | solution.py:26
  9.2 1.3 %collective-permute-start.1 = (bf16[2,512,128]{2,1,0:T(8,128)(2,1)S(1)}, bf16[2,512,128]{2,1,0:T(8,128)(2,1)S(1)}, u32[]{:S(2)}, u32[]{:S(2)}) collective-permute-start(bf16[2,512,128]{2,1,0:T(8,128)(2,1)S(1)} %get-tuple-element.28.qb_ref), channel_id=1, source_target_pairs={{4,0},{5,1},{6,2},{7,3},{8,4},{9,5},{10,6},{11,7},{12,8},{13,9},{1... | collective-permute-start | bytes 786440 | tf_op jit(solution)/shard_map/ppermute | solution.py:26
  10.5 0.0 copy-done.1
  10.5 3.8 %shard_map.65 = (f32[1024,128]{1,0:T(8,128)S(1)}, f32[1024,128]{1,0:T(8,128)S(1)}, f32[1024,128]{1,0:T(8,128)S(1)}) custom-call(s32[4]{0:T(128)S(1)} %copy-done.1, bf16[2,512,128]{2,1,0:T(8,128)(2,1)S(1)} %get-tuple-element.27.qa_ref, bf16[2,512,128]{2,1,0:T(8,128)(2,1)S(1)} %get-tuple-element.28.qb_ref, bf16[2,1024,128]{2,1,0:T(8,128)(2,1)S(1)} %get-tuple-element.29.kv_ref), custom_call_target="tpu_custom_call" | custom-call | flops 1342177280 | bytes 2621456 | tf_op jit(solution)/shard_map/pallas_call | solution.py:290
  14.3 2.8 %collective-permute-done.qan_ref = bf16[2,512,128]{2,1,0:T(8,128)(2,1)S(1)} collective-permute-done((bf16[2,512,128]{2,1,0:T(8,128)(2,1)S(1)}, bf16[2,512,128]{2,1,0:T(8,128)(2,1)S(1)}, u32[]{:S(2)}, u32[]{:S(2)}) %collective-permute-start) | collective-permute-done | bytes 262176 | tf_op jit(solution)/shard_map/ppermute | solution.py:26
  17.1 2.7 %shard_map.67 = (f32[512,128]{1,0:T(8,128)S(1)}, f32[1024,128]{1,0:T(8,128)S(1)}, f32[1024,128]{1,0:T(8,128)S(1)}) custom-call(s32[4]{0:T(128)S(1)} %copy-done.1, bf16[2,512,128]{2,1,0:T(8,128)(2,1)S(1)} %collective-permute-done.qan_ref, bf16[2,1024,128]{2,1,0:T(8,128)(2,1)S(1)} %get-tuple-element.29.kv_ref, ...), custom_call_target="tpu_custom_call", output_to_operand_aliasing={{1}: (3, {}), {2}: (4, {})} | custom-call | flops 1342177280 | bytes 3145744 | tf_op jit(solution)/shard_map/pallas_call | solution.py:290
  19.9 0.0 collective-permute-done.2.kvn_ref
  19.9 0.8 %shard_map.66 = (f32[1024,128]{1,0:T(8,128)S(1)}, f32[1024,128]{1,0:T(8,128)S(1)}, f32[1024,128]{1,0:T(8,128)S(1)}) custom-call(s32[4]{0:T(128)S(1)} %copy-done.1, bf16[2,512,128]{2,1,0:T(8,128)(2,1)S(1)} %get-tuple-element.27.qa_ref, bf16[2,512,128]{2,1,0:T(8,128)(2,1)S(1)} %get-tuple-element.28.qb_ref, ...), custom_call_target="tpu_custom_call", output_to_operand_aliasing={{0}: (4, {})} | custom-call | flops 1342177280 | bytes 3145744 | tf_op jit(solution)/shard_map/pallas_call | solution.py:290
  20.7 0.9 %collective-permute-done.1.qbn_ref = bf16[2,512,128]{2,1,0:T(8,128)(2,1)S(1)} collective-permute-done((bf16[2,512,128]{2,1,0:T(8,128)(2,1)S(1)}, bf16[2,512,128]{2,1,0:T(8,128)(2,1)S(1)}, u32[]{:S(2)}, u32[]{:S(2)}) %collective-permute-start.1) | collective-permute-done | bytes 262176 | tf_op jit(solution)/shard_map/ppermute | solution.py:26
  21.6 3.0 %shard_map.68 = (bf16[3,512,128]{2,1,0:T(8,128)(2,1)S(1)}, bf16[3,512,128]{2,1,0:T(8,128)(2,1)S(1)}, bf16[512,128]{1,0:T(8,128)(2,1)S(1)}, bf16[512,128]{1,0:T(8...) custom-call(s32[4]{0:T(128)S(1)} %copy-done.1, ...), custom_call_target="tpu_custom_call", output_to_operand_aliasing={{6}: (6, {}), {7}: (7, {}), {8}: (8, {}), {9}: (9, {}), {10... | custom-call | flops 1342177280 | bytes 8388624 | tf_op jit(solution)/shard_map/pallas_call | solution.py:290
  24.6 0.1 collective-permute-start.8
  24.7 4.3 %collective-permute-start.3 = (bf16[512,128]{1,0:T(8,128)(2,1)S(1)}, bf16[512,128]{1,0:T(8,128)(2,1)S(1)}, u32[]{:S(2)}, u32[]{:S(2)}) collective-permute-start(bf16[512,128]{1,0:T(8,128)(2,1)S(1)} %get-tuple-element.39), channel_id=1, source_target_pairs={{0,4},{1,5},{2,6},{3,7},{4,8},{5,9},{6,10},{7,11},{8,12},{9,13},{1... | collective-permute-start | bytes 393224 | tf_op jit(solution)/shard_map/ppermute | solution.py:26
  29.0 1.3 %collective-permute-start.4 = (bf16[2,512,128]{2,1,0:T(8,128)(2,1)S(1)}, bf16[2,512,128]{2,1,0:T(8,128)(2,1)S(1)}, u32[]{:S(2)}, u32[]{:S(2)}) collective-permute-start(bf16[2,512,128]{2,1,0:T(8,128)(2,1)S(1)} %get-tuple-element.40), channel_id=1, source_target_pairs={{8,0},{9,1},{10,2},{11,3},{12,4},{13,5},{14,6},{15,7},{16,8},{17,9... | collective-permute-start | bytes 786440 | tf_op jit(solution)/shard_map/ppermute | solution.py:26
  30.3 0.0 collective-permute-done.10.w2_ref
  30.3 1.3 %collective-permute-start.6 = (bf16[2,512,128]{2,1,0:T(8,128)(2,1)S(1)}, bf16[2,512,128]{2,1,0:T(8,128)(2,1)S(1)}, u32[]{:S(2)}, u32[]{:S(2)}) collective-permute-start(bf16[2,512,128]{2,1,0:T(8,128)(2,1)S(1)} %get-tuple-element.42), channel_id=1, source_target_pairs={{8,2},{9,3},{10,0},{11,1},{12,6},{13,7},{14,4},{15,5},{16,10},{17,... | collective-permute-start | bytes 786440 | tf_op jit(solution)/shard_map/ppermute | solution.py:26
  31.6 0.8 %collective-permute-done.3.dq_same = bf16[512,128]{1,0:T(8,128)(2,1)S(1)} collective-permute-done((bf16[512,128]{1,0:T(8,128)(2,1)S(1)}, bf16[512,128]{1,0:T(8,128)(2,1)S(1)}, u32[]{:S(2)}, u32[]{:S(2)}) %collective-permute-start.3) | collective-permute-done | bytes 131104 | tf_op jit(solution)/shard_map/ppermute | solution.py:26
  32.4 5.3 %collective-permute-start.5 = (bf16[512,128]{1,0:T(8,128)(2,1)S(1)}, bf16[512,128]{1,0:T(8,128)(2,1)S(1)}, u32[]{:S(2)}, u32[]{:S(2)}) collective-permute-start(bf16[512,128]{1,0:T(8,128)(2,1)S(1)} %get-tuple-element.41), channel_id=1, source_target_pairs={{0,6},{1,7},{2,4},{3,5},{4,10},{5,11},{6,8},{7,9},{8,14},{9,15},{1... | collective-permute-start | bytes 393224 | tf_op jit(solution)/shard_map/ppermute | solution.py:26
  37.7 8.1 %collective-permute-done.5.dq_cross = bf16[512,128]{1,0:T(8,128)(2,1)S(1)} collective-permute-done((bf16[512,128]{1,0:T(8,128)(2,1)S(1)}, bf16[512,128]{1,0:T(8,128)(2,1)S(1)}, u32[]{:S(2)}, u32[]{:S(2)}) %collective-permute-start.5) | collective-permute-done | bytes 131104 | tf_op jit(solution)/shard_map/ppermute | solution.py:26
  45.9 0.0 collective-permute-start.12
  45.9 0.0 collective-permute-done.4.dkv_same
  45.9 0.1 collective-permute-done.6.dkv_cross
  46.0 0.1 shard_map.69
  46.0 0.5 collective-permute-start.7
  46.5 0.0 collective-permute-done.9.w1_ref
  46.5 0.0 collective-permute-done.8.got_ref
  46.5 0.6 %shard_map.70 = (f32[256,512]{1,0:T(8,128)S(1)}, bf16[256,512]{1,0:T(8,128)(2,1)S(1)}) custom-call(bf16[3,512,128]{2,1,0:T(8,128)(2,1)S(1)} %get-tuple-element.45.keep_ref, bf16[3,512,128]{2,1,0:T(8,128)(2,1)S(1)} %collective-permute-done.8.got_ref, bf16[3,512,128]{2,1,0:T(8,128)(2,1)S(1)} %copy-done, bf16[3,512,128]{2,1,0:T(8,128)(2,1)S(1)} %collective-permute-done.9.w1_ref), custom_call_target="tpu_custom_call" | custom-call | flops 201326592 | bytes 2359296 | tf_op jit(solution)/shard_map/pallas_call | solution.py:290
  47.1 0.6 %collective-permute-start.11 = (bf16[256,512]{1,0:T(8,128)(2,1)S(1)}, bf16[256,512]{1,0:T(8,128)(2,1)S(1)}, u32[]{:S(2)}, u32[]{:S(2)}) collective-permute-start(bf16[256,512]{1,0:T(8,128)(2,1)S(1)} %get-tuple-element.48), channel_id=1, source_target_pairs={{0,2},{1,3},{2,0},{3,1},{4,6},{5,7},{6,4},{7,5},{8,10},{9,11},{10,... | collective-permute-start | bytes 786440 | tf_op jit(solution)/shard_map/ppermute | solution.py:26
  47.7 0.4 shard_map.71.partial_ref
  48.1 0.0 collective-permute-done.12.w3_ref
  48.1 0.0 collective-permute-done.7.got_ref
  48.2 7.4 %collective-permute-done.11.arrived_ref = bf16[256,512]{1,0:T(8,128)(2,1)S(1)} collective-permute-done((bf16[256,512]{1,0:T(8,128)(2,1)S(1)}, bf16[256,512]{1,0:T(8,128)(2,1)S(1)}, u32[]{:S(2)}, u32[]{:S(2)}) %collective-permute-start.11) | collective-permute-done | bytes 262176 | tf_op jit(solution)/shard_map/ppermute | solution.py:26
  55.5 1.2 %shard_map.72 = f32[256,512]{1,0:T(8,128)} custom-call(bf16[2,3,256,128]{3,2,1,0:T(8,128)(2,1)S(1)} %collective-permute-done.7.got_ref, f32[256,512]{1,0:T(8,128)S(1)} %shard_map.71.partial_ref, bf16[256,512]{1,0:T(8,128)(2,1)S(1)} %collective-permute-done.11.arrived_ref, bf16[3,512,128]{2,1,0:T(8,128)(2,1)S(1)} %collective-permute-done.9.w1_ref, ...), custom_call_target="tpu_custom_call" | custom-call | flops 201326592 | bytes 2490368 | tf_op jit(solution)/shard_map/pallas_call | solution.py:290
Async XLA Ops:
  0.0 7.6 %copy-start = (bf16[3,512,128]{2,1,0:T(8,128)(2,1)S(1)}, bf16[3,512,128]{2,1,0:T(8,128)(2,1)}, u32[]{:S(2)}) copy-start(bf16[3,512,128]{2,1,0:T(8,128)(2,1)} %w_ref.3) | copy-start | bytes 1179652
  1.3 18.6 %collective-permute-start.2 = (bf16[2,1024,128]{2,1,0:T(8,128)(2,1)S(1)}, bf16[2,1024,128]{2,1,0:T(8,128)(2,1)S(1)}, u32[]{:S(2)}, u32[]{:S(2)}) collective-permute-start(bf16[2,1024,128]{2,1,0:T(8,128)(2,1)S(1)} %get-tuple-element.29.kv_ref), channel_id=1, source_target_pairs={{0,8},{1,9},{2,10},{3,11},{4,12},{5,13},{6,14},{7,15},{8,16},{9,17... | collective-permute-start | bytes 1572872 | tf_op jit(solution)/shard_map/ppermute | solution.py:26
  6.3 4.2 %copy-start.1 = (s32[4]{0:T(128)S(1)}, s32[4]{0:T(128)}, u32[]{:S(2)}) copy-start(s32[4]{0:T(128)} %lengths_ref.7) | copy-start | bytes 52
  6.3 10.8 %collective-permute-start = (bf16[2,512,128]{2,1,0:T(8,128)(2,1)S(1)}, bf16[2,512,128]{2,1,0:T(8,128)(2,1)S(1)}, u32[]{:S(2)}, u32[]{:S(2)}) collective-permute-start(bf16[2,512,128]{2,1,0:T(8,128)(2,1)S(1)} %get-tuple-element.27.qa_ref), channel_id=1, source_target_pairs={{4,0},{5,1},{6,2},{7,3},{8,4},{9,5},{10,6},{11,7},{12,8},{13,9},{1... | collective-permute-start | bytes 786440 | tf_op jit(solution)/shard_map/ppermute | solution.py:26
  7.6 38.9 %collective-permute-start.9 = (bf16[3,512,128]{2,1,0:T(8,128)(2,1)S(1)}, bf16[3,512,128]{2,1,0:T(8,128)(2,1)S(1)}, u32[]{:S(2)}, u32[]{:S(2)}) collective-permute-start(bf16[3,512,128]{2,1,0:T(8,128)(2,1)S(1)} %copy-done), channel_id=1, source_target_pairs={{0,1},{1,0},{2,3},{3,2},{4,5},{5,4},{6,7},{7,6},{8,9},{9,8},{10,11... | collective-permute-start | bytes 1179656 | tf_op jit(solution)/shard_map/ppermute | solution.py:26
  7.7 22.6 %collective-permute-start.10 = (bf16[3,512,128]{2,1,0:T(8,128)(2,1)S(1)}, bf16[3,512,128]{2,1,0:T(8,128)(2,1)S(1)}, u32[]{:S(2)}, u32[]{:S(2)}) collective-permute-start(bf16[3,512,128]{2,1,0:T(8,128)(2,1)S(1)} %copy-done), channel_id=1, source_target_pairs={{0,2},{1,3},{2,0},{3,1},{4,6},{5,7},{6,4},{7,5},{8,10},{9,11},{10,... | collective-permute-start | bytes 1179656 | tf_op jit(solution)/shard_map/ppermute | solution.py:26
  9.2 12.3 %collective-permute-start.1 = (bf16[2,512,128]{2,1,0:T(8,128)(2,1)S(1)}, bf16[2,512,128]{2,1,0:T(8,128)(2,1)S(1)}, u32[]{:S(2)}, u32[]{:S(2)}) collective-permute-start(bf16[2,512,128]{2,1,0:T(8,128)(2,1)S(1)} %get-tuple-element.28.qb_ref), channel_id=1, source_target_pairs={{4,0},{5,1},{6,2},{7,3},{8,4},{9,5},{10,6},{11,7},{12,8},{13,9},{1... | collective-permute-start | bytes 786440 | tf_op jit(solution)/shard_map/ppermute | solution.py:26
  24.6 21.9 %collective-permute-start.8 = (bf16[3,512,128]{2,1,0:T(8,128)(2,1)S(1)}, bf16[3,512,128]{2,1,0:T(8,128)(2,1)S(1)}, u32[]{:S(2)}, u32[]{:S(2)}) collective-permute-start(bf16[3,512,128]{2,1,0:T(8,128)(2,1)S(1)} %get-tuple-element.46), channel_id=1, source_target_pairs={{0,1},{1,0},{2,3},{3,2},{4,5},{5,4},{6,7},{7,6},{8,9},{9,8},{10,11... | collective-permute-start | bytes 1179656 | tf_op jit(solution)/shard_map/ppermute | solution.py:26
  24.7 7.7 %collective-permute-start.3 = (bf16[512,128]{1,0:T(8,128)(2,1)S(1)}, bf16[512,128]{1,0:T(8,128)(2,1)S(1)}, u32[]{:S(2)}, u32[]{:S(2)}) collective-permute-start(bf16[512,128]{1,0:T(8,128)(2,1)S(1)} %get-tuple-element.39), channel_id=1, source_target_pairs={{0,4},{1,5},{2,6},{3,7},{4,8},{5,9},{6,10},{7,11},{8,12},{9,13},{1... | collective-permute-start | bytes 393224 | tf_op jit(solution)/shard_map/ppermute | solution.py:26
  29.0 16.8 %collective-permute-start.4 = (bf16[2,512,128]{2,1,0:T(8,128)(2,1)S(1)}, bf16[2,512,128]{2,1,0:T(8,128)(2,1)S(1)}, u32[]{:S(2)}, u32[]{:S(2)}) collective-permute-start(bf16[2,512,128]{2,1,0:T(8,128)(2,1)S(1)} %get-tuple-element.40), channel_id=1, source_target_pairs={{8,0},{9,1},{10,2},{11,3},{12,4},{13,5},{14,6},{15,7},{16,8},{17,9... | collective-permute-start | bytes 786440 | tf_op jit(solution)/shard_map/ppermute | solution.py:26
  30.3 15.6 %collective-permute-start.6 = (bf16[2,512,128]{2,1,0:T(8,128)(2,1)S(1)}, bf16[2,512,128]{2,1,0:T(8,128)(2,1)S(1)}, u32[]{:S(2)}, u32[]{:S(2)}) collective-permute-start(bf16[2,512,128]{2,1,0:T(8,128)(2,1)S(1)} %get-tuple-element.42), channel_id=1, source_target_pairs={{8,2},{9,3},{10,0},{11,1},{12,6},{13,7},{14,4},{15,5},{16,10},{17,... | collective-permute-start | bytes 786440 | tf_op jit(solution)/shard_map/ppermute | solution.py:26
  32.4 13.5 %collective-permute-start.5 = (bf16[512,128]{1,0:T(8,128)(2,1)S(1)}, bf16[512,128]{1,0:T(8,128)(2,1)S(1)}, u32[]{:S(2)}, u32[]{:S(2)}) collective-permute-start(bf16[512,128]{1,0:T(8,128)(2,1)S(1)} %get-tuple-element.41), channel_id=1, source_target_pairs={{0,6},{1,7},{2,4},{3,5},{4,10},{5,11},{6,8},{7,9},{8,14},{9,15},{1... | collective-permute-start | bytes 393224 | tf_op jit(solution)/shard_map/ppermute | solution.py:26
  45.9 2.3 %collective-permute-start.12 = (bf16[3,512,128]{2,1,0:T(8,128)(2,1)S(1)}, bf16[3,512,128]{2,1,0:T(8,128)(2,1)S(1)}, u32[]{:S(2)}, u32[]{:S(2)}) collective-permute-start(bf16[3,512,128]{2,1,0:T(8,128)(2,1)S(1)} %collective-permute-done.10.w2_ref), channel_id=1, source_target_pairs={{0,1},{1,0},{2,3},{3,2},{4,5},{5,4},{6,7},{7,6},{8,9},{9,8},{10,11... | collective-permute-start | bytes 1179656 | tf_op jit(solution)/shard_map/ppermute | solution.py:26
  46.0 2.1 %collective-permute-start.7 = (bf16[2,3,256,128]{3,2,1,0:T(8,128)(2,1)S(1)}, bf16[2,3,256,128]{3,2,1,0:T(8,128)(2,1)S(1)}, u32[]{:S(2)}, u32[]{:S(2)}) collective-permute-start(bf16[2,3,256,128]{3,2,1,0:T(8,128)(2,1)S(1)} %get-tuple-element.43), channel_id=1, source_target_pairs={{0,1},{1,0},{2,3},{3,2},{4,5},{5,4},{6,7},{7,6},{8,9},{9,8},{10,11... | collective-permute-start | bytes 1179656 | tf_op jit(solution)/shard_map/ppermute | solution.py:26
  47.1 8.4 %collective-permute-start.11 = (bf16[256,512]{1,0:T(8,128)(2,1)S(1)}, bf16[256,512]{1,0:T(8,128)(2,1)S(1)}, u32[]{:S(2)}, u32[]{:S(2)}) collective-permute-start(bf16[256,512]{1,0:T(8,128)(2,1)S(1)} %get-tuple-element.48), channel_id=1, source_target_pairs={{0,2},{1,3},{2,0},{3,1},{4,6},{5,7},{6,4},{7,5},{8,10},{9,11},{10,... | collective-permute-start | bytes 786440 | tf_op jit(solution)/shard_map/ppermute | solution.py:26

commit v3 on v2

--- a/solution.py
+++ b/solution.py
@@ -258,13 +258,18 @@
         out_ref[...] = project(grads, weights).astype(out_ref.dtype)
 
 
-def split_kernel(dq_same, dkv_same, dq_cross, dkv_cross, keep_ref, send_ref):
+def pair_kernel(same_ref, partner_ref, out_ref):
+    out_ref[0] = same_ref[...]
+    out_ref[1] = partner_ref[...]
+
+
+def split_kernel(dq_pair, dkv_same, dkv_cross, keep_ref, send_ref):
     block = keep_ref.shape[2]
     low = lax.axis_index("head") % 2
     for bit, out_ref in ((1 - low, send_ref), (low, keep_ref)):
         src = pl.ds(pl.multiple_of(bit * block, block), block)
-        for n, (dq, dkv) in enumerate(((dq_same, dkv_same), (dq_cross, dkv_cross))):
-            out_ref[n, 0] = dq[src, :]
+        for n, dkv in enumerate((dkv_same, dkv_cross)):
+            out_ref[n, 0] = dq_pair[n, src, :]
             out_ref[n, 1] = dkv[0, src, :]
             out_ref[n, 2] = dkv[1, src, :]
 
@@ -347,10 +352,14 @@
         aliases=((6, 6), (7, 7), (8, 8), (9, 9), (10, 10)),
     )
     w1, w3 = shift(w_proj, 0, 1), shift(w2, 0, 1)
+    partner = shift(dq_cross, 0, 2)
+    (dq_pair,) = call(
+        pair_kernel, (like((2, rows // 2, width), BF16),), (dq_same, partner), 1000,
+        lengths=False,
+    )
+    dq_pair = shift(dq_pair, 1)
     dkv_cross = shift(dkv_cross, -2, 2)
     dkv_same = shift(dkv_same, -2)
-    dq_cross = shift(dq_cross, 1, 2)
-    dq_same = shift(dq_same, 1)
     got = shift(send, 0, 1)
     mine, send = call(
         local_kernel, (like((block, model), F32), like((block, model), BF16)),
@@ -360,7 +369,7 @@
 
     quarter = like((2, 3, block, width), BF16)
     keep, send = call(
-        split_kernel, (quarter, quarter), (dq_same, dkv_same, dq_cross, dkv_cross), 1000,
+        split_kernel, (quarter, quarter), (dq_pair, dkv_same, dkv_cross), 1000,
         lengths=False,
     )
     got = shift(send, 0, 1)

time: 57.2 us -> 53.3 us (0.932)
  starting transfers between devices: 22.5 us -> 19.7 us
  waiting for transfers between devices: 20.1 us -> 19.2 us
    ppermute x13, starting transfers between devices: 22.5 us -> 19.7 us  [shift(): return lax.ppermute(value, ('seq', 'head'), pairs)]
    ppermute x13, waiting for transfers between devices: 20.1 us -> 19.2 us  [shift(): return lax.ppermute(value, ('seq', 'head'), pairs)]
    pallas_call x9 -> x10, Pallas kernels: 13.9 us -> 13.9 us  [call(): pl.pallas_call(body, out_shape=outs, in_specs=specs, out_specs=tuple((VME...]
  transfers between devices with their start and end apart: 13 -> 13, of which waited for: 6 -> 6; matrix products, arithmetic and copies ran while one was open for 0% -> 0% of each run, Pallas kernels for 20% -> 22%
where the time goes in v3:
time: 53.3 us; the launch traced here: 53.1 us
  starting transfers between devices  19.7 us (37%)
  waiting for transfers between devices  19.2 us (36%)
  Pallas kernels  13.9 us (26%)
    ppermute x13, starting transfers between devices, shift(): return lax.ppermute(value, ('seq', 'head'), pairs)  19.7 us
    ppermute x13, waiting for transfers between devices, shift(): return lax.ppermute(value, ('seq', 'head'), pairs)  19.2 us
    pallas_call x10, Pallas kernels, call(): pl.pallas_call(body, out_shape=outs, in_specs=specs, out_specs=tuple((VME...  13.9 us
  transfers between devices with their start and end apart: 13, of which 6 were waited for; matrix products, arithmetic and copies ran while one was open for 0% of the time, Pallas kernels for 22%

profile of v3, /device:TPU:0, one launch (start us, length us, event | category | flops | bytes accessed | tf_op | source)
XLA Modules:
  0.0 53.1 jit_solution(11505491101792998892)
XLA Ops:
  0.0 0.0 copy-start
  0.0 1.3 %shard_map.64 = (bf16[2,512,128]{2,1,0:T(8,128)(2,1)S(1)}, bf16[2,512,128]{2,1,0:T(8,128)(2,1)S(1)}, bf16[2,1024,128]{2,1,0:T(8,128)(2,1)S(1)}) custom-call(bf16[1024,128]{1,0:T(8,128)(2,1)} %q_hbm.1, bf16[1024,128]{1,0:T(8,128)(2,1)} %g_hbm.1, bf16[1024,128]{1,0:T(8,128)(2,1)} %k_hbm.1, bf16[1024,128]{1,0:T(8,128)(2,1)} %v_hbm.1), custom_call_target="tpu_custom_call" | custom-call | flops 1000 | bytes 2097152 | tf_op jit(solution)/shard_map/pallas_call | solution.py:295
  1.3 5.0 %collective-permute-start.2 = (bf16[2,1024,128]{2,1,0:T(8,128)(2,1)S(1)}, bf16[2,1024,128]{2,1,0:T(8,128)(2,1)S(1)}, u32[]{:S(2)}, u32[]{:S(2)}) collective-permute-start(bf16[2,1024,128]{2,1,0:T(8,128)(2,1)S(1)} %get-tuple-element.29.kv_ref), channel_id=1, source_target_pairs={{0,8},{1,9},{2,10},{3,11},{4,12},{5,13},{6,14},{7,15},{8,16},{9,17... | collective-permute-start | bytes 1572872 | tf_op jit(solution)/shard_map/ppermute | solution.py:26
  6.3 0.0 copy-start.1
  6.3 1.3 %collective-permute-start = (bf16[2,512,128]{2,1,0:T(8,128)(2,1)S(1)}, bf16[2,512,128]{2,1,0:T(8,128)(2,1)S(1)}, u32[]{:S(2)}, u32[]{:S(2)}) collective-permute-start(bf16[2,512,128]{2,1,0:T(8,128)(2,1)S(1)} %get-tuple-element.27.qa_ref), channel_id=1, source_target_pairs={{4,0},{5,1},{6,2},{7,3},{8,4},{9,5},{10,6},{11,7},{12,8},{13,9},{1... | collective-permute-start | bytes 786440 | tf_op jit(solution)/shard_map/ppermute | solution.py:26
  7.6 1.3 %collective-permute-start.1 = (bf16[2,512,128]{2,1,0:T(8,128)(2,1)S(1)}, bf16[2,512,128]{2,1,0:T(8,128)(2,1)S(1)}, u32[]{:S(2)}, u32[]{:S(2)}) collective-permute-start(bf16[2,512,128]{2,1,0:T(8,128)(2,1)S(1)} %get-tuple-element.28.qb_ref), channel_id=1, source_target_pairs={{4,0},{5,1},{6,2},{7,3},{8,4},{9,5},{10,6},{11,7},{12,8},{13,9},{1... | collective-permute-start | bytes 786440 | tf_op jit(solution)/shard_map/ppermute | solution.py:26
  8.9 0.0 copy-done
  8.9 1.6 %collective-permute-start.10 = (bf16[3,512,128]{2,1,0:T(8,128)(2,1)S(1)}, bf16[3,512,128]{2,1,0:T(8,128)(2,1)S(1)}, u32[]{:S(2)}, u32[]{:S(2)}) collective-permute-start(bf16[3,512,128]{2,1,0:T(8,128)(2,1)S(1)} %copy-done), channel_id=1, source_target_pairs={{0,2},{1,3},{2,0},{3,1},{4,6},{5,7},{6,4},{7,5},{8,10},{9,11},{10,... | collective-permute-start | bytes 1179656 | tf_op jit(solution)/shard_map/ppermute | solution.py:26
  10.5 0.0 copy-done.1
  10.5 3.8 %shard_map.65 = (f32[1024,128]{1,0:T(8,128)S(1)}, f32[1024,128]{1,0:T(8,128)S(1)}, f32[1024,128]{1,0:T(8,128)S(1)}) custom-call(s32[4]{0:T(128)S(1)} %copy-done.1, bf16[2,512,128]{2,1,0:T(8,128)(2,1)S(1)} %get-tuple-element.27.qa_ref, bf16[2,512,128]{2,1,0:T(8,128)(2,1)S(1)} %get-tuple-element.28.qb_ref, bf16[2,1024,128]{2,1,0:T(8,128)(2,1)S(1)} %get-tuple-element.29.kv_ref), custom_call_target="tpu_custom_call" | custom-call | flops 1342177280 | bytes 2621456 | tf_op jit(solution)/shard_map/pallas_call | solution.py:295
  14.3 3.1 %collective-permute-done.qan_ref = bf16[2,512,128]{2,1,0:T(8,128)(2,1)S(1)} collective-permute-done((bf16[2,512,128]{2,1,0:T(8,128)(2,1)S(1)}, bf16[2,512,128]{2,1,0:T(8,128)(2,1)S(1)}, u32[]{:S(2)}, u32[]{:S(2)}) %collective-permute-start) | collective-permute-done | bytes 262176 | tf_op jit(solution)/shard_map/ppermute | solution.py:26
  17.4 2.7 %shard_map.67 = (f32[512,128]{1,0:T(8,128)S(1)}, f32[1024,128]{1,0:T(8,128)S(1)}, f32[1024,128]{1,0:T(8,128)S(1)}) custom-call(s32[4]{0:T(128)S(1)} %copy-done.1, bf16[2,512,128]{2,1,0:T(8,128)(2,1)S(1)} %collective-permute-done.qan_ref, bf16[2,1024,128]{2,1,0:T(8,128)(2,1)S(1)} %get-tuple-element.29.kv_ref, ...), custom_call_target="tpu_custom_call", output_to_operand_aliasing={{1}: (3, {}), {2}: (4, {})} | custom-call | flops 1342177280 | bytes 3145744 | tf_op jit(solution)/shard_map/pallas_call | solution.py:295
  20.1 0.0 collective-permute-done.2.kvn_ref
  20.1 0.8 %shard_map.66 = (f32[1024,128]{1,0:T(8,128)S(1)}, f32[1024,128]{1,0:T(8,128)S(1)}, f32[1024,128]{1,0:T(8,128)S(1)}) custom-call(s32[4]{0:T(128)S(1)} %copy-done.1, bf16[2,512,128]{2,1,0:T(8,128)(2,1)S(1)} %get-tuple-element.27.qa_ref, bf16[2,512,128]{2,1,0:T(8,128)(2,1)S(1)} %get-tuple-element.28.qb_ref, ...), custom_call_target="tpu_custom_call", output_to_operand_aliasing={{0}: (4, {})} | custom-call | flops 1342177280 | bytes 3145744 | tf_op jit(solution)/shard_map/pallas_call | solution.py:295
  21.0 0.6 %collective-permute-done.1.qbn_ref = bf16[2,512,128]{2,1,0:T(8,128)(2,1)S(1)} collective-permute-done((bf16[2,512,128]{2,1,0:T(8,128)(2,1)S(1)}, bf16[2,512,128]{2,1,0:T(8,128)(2,1)S(1)}, u32[]{:S(2)}, u32[]{:S(2)}) %collective-permute-start.1) | collective-permute-done | bytes 262176 | tf_op jit(solution)/shard_map/ppermute | solution.py:26
  21.6 3.0 %shard_map.68 = (bf16[3,512,128]{2,1,0:T(8,128)(2,1)S(1)}, bf16[3,512,128]{2,1,0:T(8,128)(2,1)S(1)}, bf16[512,128]{1,0:T(8,128)(2,1)S(1)}, bf16[512,128]{1,0:T(8...) custom-call(s32[4]{0:T(128)S(1)} %copy-done.1, ...), custom_call_target="tpu_custom_call", output_to_operand_aliasing={{6}: (6, {}), {7}: (7, {}), {8}: (8, {}), {9}: (9, {}), {10... | custom-call | flops 1342177280 | bytes 8388624 | tf_op jit(solution)/shard_map/pallas_call | solution.py:295
  24.6 1.6 %collective-permute-start.3 = (bf16[512,128]{1,0:T(8,128)(2,1)S(1)}, bf16[512,128]{1,0:T(8,128)(2,1)S(1)}, u32[]{:S(2)}, u32[]{:S(2)}) collective-permute-start(bf16[512,128]{1,0:T(8,128)(2,1)S(1)} %get-tuple-element.40), channel_id=1, source_target_pairs={{0,2},{1,3},{2,0},{3,1},{4,6},{5,7},{6,4},{7,5},{8,10},{9,11},{10,... | collective-permute-start | bytes 393224 | tf_op jit(solution)/shard_map/ppermute | solution.py:26
  26.2 0.0 collective-permute-start.9
  26.2 0.5 collective-permute-start.8
  26.7 1.3 %collective-permute-start.5 = (bf16[2,512,128]{2,1,0:T(8,128)(2,1)S(1)}, bf16[2,512,128]{2,1,0:T(8,128)(2,1)S(1)}, u32[]{:S(2)}, u32[]{:S(2)}) collective-permute-start(bf16[2,512,128]{2,1,0:T(8,128)(2,1)S(1)} %get-tuple-element.41), channel_id=1, source_target_pairs={{8,0},{9,1},{10,2},{11,3},{12,4},{13,5},{14,6},{15,7},{16,8},{17,9... | collective-permute-start | bytes 786440 | tf_op jit(solution)/shard_map/ppermute | solution.py:26
  28.0 1.7 %collective-permute-done.3.partner_ref = bf16[512,128]{1,0:T(8,128)(2,1)S(1)} collective-permute-done((bf16[512,128]{1,0:T(8,128)(2,1)S(1)}, bf16[512,128]{1,0:T(8,128)(2,1)S(1)}, u32[]{:S(2)}, u32[]{:S(2)}) %collective-permute-start.3) | collective-permute-done | bytes 131104 | tf_op jit(solution)/shard_map/ppermute | solution.py:26
  29.6 1.3 %collective-permute-start.6 = (bf16[2,512,128]{2,1,0:T(8,128)(2,1)S(1)}, bf16[2,512,128]{2,1,0:T(8,128)(2,1)S(1)}, u32[]{:S(2)}, u32[]{:S(2)}) collective-permute-start(bf16[2,512,128]{2,1,0:T(8,128)(2,1)S(1)} %get-tuple-element.42), channel_id=1, source_target_pairs={{8,2},{9,3},{10,0},{11,1},{12,6},{13,7},{14,4},{15,5},{16,10},{17,... | collective-permute-start | bytes 786440 | tf_op jit(solution)/shard_map/ppermute | solution.py:26
  31.0 0.0 collective-permute-done.10.w2_ref
  31.0 4.3 %collective-permute-start.4 = (bf16[2,512,128]{2,1,0:T(8,128)(2,1)S(1)}, bf16[2,512,128]{2,1,0:T(8,128)(2,1)S(1)}, u32[]{:S(2)}, u32[]{:S(2)}) collective-permute-start(bf16[2,512,128]{2,1,0:T(8,128)(2,1)S(1)} %shard_map.69), channel_id=1, source_target_pairs={{0,4},{1,5},{2,6},{3,7},{4,8},{5,9},{6,10},{7,11},{8,12},{9,13},{1... | collective-permute-start | bytes 786440 | tf_op jit(solution)/shard_map/ppermute | solution.py:26
  35.3 2.4 %collective-permute-done.5.dkv_same = bf16[2,512,128]{2,1,0:T(8,128)(2,1)S(1)} collective-permute-done((bf16[2,512,128]{2,1,0:T(8,128)(2,1)S(1)}, bf16[2,512,128]{2,1,0:T(8,128)(2,1)S(1)}, u32[]{:S(2)}, u32[]{:S(2)}) %collective-permute-start.5) | collective-permute-done | bytes 262176 | tf_op jit(solution)/shard_map/ppermute | solution.py:26
  37.7 0.0 collective-permute-start.12
  37.8 4.6 %collective-permute-done.6.dkv_cross = bf16[2,512,128]{2,1,0:T(8,128)(2,1)S(1)} collective-permute-done((bf16[2,512,128]{2,1,0:T(8,128)(2,1)S(1)}, bf16[2,512,128]{2,1,0:T(8,128)(2,1)S(1)}, u32[]{:S(2)}, u32[]{:S(2)}) %collective-permute-start.6) | collective-permute-done | bytes 262176 | tf_op jit(solution)/shard_map/ppermute | solution.py:26
  42.4 0.0 collective-permute-done.4.dq_pair
  42.4 0.1 shard_map.70
  42.4 0.1 collective-permute-start.7
  42.5 0.0 collective-permute-done.9.w1_ref
  42.5 0.0 collective-permute-done.8.got_ref
  42.5 0.6 %shard_map.71 = (f32[256,512]{1,0:T(8,128)S(1)}, bf16[256,512]{1,0:T(8,128)(2,1)S(1)}) custom-call(bf16[3,512,128]{2,1,0:T(8,128)(2,1)S(1)} %get-tuple-element.45.keep_ref, bf16[3,512,128]{2,1,0:T(8,128)(2,1)S(1)} %collective-permute-done.8.got_ref, bf16[3,512,128]{2,1,0:T(8,128)(2,1)S(1)} %copy-done, bf16[3,512,128]{2,1,0:T(8,128)(2,1)S(1)} %collective-permute-done.9.w1_ref), custom_call_target="tpu_custom_call" | custom-call | flops 201326592 | bytes 2359296 | tf_op jit(solution)/shard_map/pallas_call | solution.py:295
  43.1 1.6 %collective-permute-start.11 = (bf16[256,512]{1,0:T(8,128)(2,1)S(1)}, bf16[256,512]{1,0:T(8,128)(2,1)S(1)}, u32[]{:S(2)}, u32[]{:S(2)}) collective-permute-start(bf16[256,512]{1,0:T(8,128)(2,1)S(1)} %get-tuple-element.48), channel_id=1, source_target_pairs={{0,2},{1,3},{2,0},{3,1},{4,6},{5,7},{6,4},{7,5},{8,10},{9,11},{10,... | collective-permute-start | bytes 786440 | tf_op jit(solution)/shard_map/ppermute | solution.py:26
  44.7 0.4 shard_map.72.partial_ref
  45.1 0.0 collective-permute-done.12.w3_ref
  45.1 6.8 %collective-permute-done.11.arrived_ref = bf16[256,512]{1,0:T(8,128)(2,1)S(1)} collective-permute-done((bf16[256,512]{1,0:T(8,128)(2,1)S(1)}, bf16[256,512]{1,0:T(8,128)(2,1)S(1)}, u32[]{:S(2)}, u32[]{:S(2)}) %collective-permute-start.11) | collective-permute-done | bytes 262176 | tf_op jit(solution)/shard_map/ppermute | solution.py:26
  51.9 0.0 collective-permute-done.7.got_ref
  51.9 1.2 %shard_map.73 = f32[256,512]{1,0:T(8,128)} custom-call(bf16[2,3,256,128]{3,2,1,0:T(8,128)(2,1)S(1)} %collective-permute-done.7.got_ref, f32[256,512]{1,0:T(8,128)S(1)} %shard_map.72.partial_ref, bf16[256,512]{1,0:T(8,128)(2,1)S(1)} %collective-permute-done.11.arrived_ref, bf16[3,512,128]{2,1,0:T(8,128)(2,1)S(1)} %collective-permute-done.9.w1_ref, ...), custom_call_target="tpu_custom_call" | custom-call | flops 201326592 | bytes 2490368 | tf_op jit(solution)/shard_map/pallas_call | solution.py:295
  (1 shorter events, 0.0 us)
Async XLA Ops:
  0.0 8.9 %copy-start = (bf16[3,512,128]{2,1,0:T(8,128)(2,1)S(1)}, bf16[3,512,128]{2,1,0:T(8,128)(2,1)}, u32[]{:S(2)}) copy-start(bf16[3,512,128]{2,1,0:T(8,128)(2,1)} %w_ref.3) | copy-start | bytes 1179652
  1.3 18.8 %collective-permute-start.2 = (bf16[2,1024,128]{2,1,0:T(8,128)(2,1)S(1)}, bf16[2,1024,128]{2,1,0:T(8,128)(2,1)S(1)}, u32[]{:S(2)}, u32[]{:S(2)}) collective-permute-start(bf16[2,1024,128]{2,1,0:T(8,128)(2,1)S(1)} %get-tuple-element.29.kv_ref), channel_id=1, source_target_pairs={{0,8},{1,9},{2,10},{3,11},{4,12},{5,13},{6,14},{7,15},{8,16},{9,17... | collective-permute-start | bytes 1572872 | tf_op jit(solution)/shard_map/ppermute | solution.py:26
  6.3 4.2 %copy-start.1 = (s32[4]{0:T(128)S(1)}, s32[4]{0:T(128)}, u32[]{:S(2)}) copy-start(s32[4]{0:T(128)} %lengths_ref.7) | copy-start | bytes 52
  6.3 11.1 %collective-permute-start = (bf16[2,512,128]{2,1,0:T(8,128)(2,1)S(1)}, bf16[2,512,128]{2,1,0:T(8,128)(2,1)S(1)}, u32[]{:S(2)}, u32[]{:S(2)}) collective-permute-start(bf16[2,512,128]{2,1,0:T(8,128)(2,1)S(1)} %get-tuple-element.27.qa_ref), channel_id=1, source_target_pairs={{4,0},{5,1},{6,2},{7,3},{8,4},{9,5},{10,6},{11,7},{12,8},{13,9},{1... | collective-permute-start | bytes 786440 | tf_op jit(solution)/shard_map/ppermute | solution.py:26
  7.6 14.0 %collective-permute-start.1 = (bf16[2,512,128]{2,1,0:T(8,128)(2,1)S(1)}, bf16[2,512,128]{2,1,0:T(8,128)(2,1)S(1)}, u32[]{:S(2)}, u32[]{:S(2)}) collective-permute-start(bf16[2,512,128]{2,1,0:T(8,128)(2,1)S(1)} %get-tuple-element.28.qb_ref), channel_id=1, source_target_pairs={{4,0},{5,1},{6,2},{7,3},{8,4},{9,5},{10,6},{11,7},{12,8},{13,9},{1... | collective-permute-start | bytes 786440 | tf_op jit(solution)/shard_map/ppermute | solution.py:26
  8.9 22.1 %collective-permute-start.10 = (bf16[3,512,128]{2,1,0:T(8,128)(2,1)S(1)}, bf16[3,512,128]{2,1,0:T(8,128)(2,1)S(1)}, u32[]{:S(2)}, u32[]{:S(2)}) collective-permute-start(bf16[3,512,128]{2,1,0:T(8,128)(2,1)S(1)} %copy-done), channel_id=1, source_target_pairs={{0,2},{1,3},{2,0},{3,1},{4,6},{5,7},{6,4},{7,5},{8,10},{9,11},{10,... | collective-permute-start | bytes 1179656 | tf_op jit(solution)/shard_map/ppermute | solution.py:26
  24.6 5.0 %collective-permute-start.3 = (bf16[512,128]{1,0:T(8,128)(2,1)S(1)}, bf16[512,128]{1,0:T(8,128)(2,1)S(1)}, u32[]{:S(2)}, u32[]{:S(2)}) collective-permute-start(bf16[512,128]{1,0:T(8,128)(2,1)S(1)} %get-tuple-element.40), channel_id=1, source_target_pairs={{0,2},{1,3},{2,0},{3,1},{4,6},{5,7},{6,4},{7,5},{8,10},{9,11},{10,... | collective-permute-start | bytes 393224 | tf_op jit(solution)/shard_map/ppermute | solution.py:26
  26.2 16.3 %collective-permute-start.9 = (bf16[3,512,128]{2,1,0:T(8,128)(2,1)S(1)}, bf16[3,512,128]{2,1,0:T(8,128)(2,1)S(1)}, u32[]{:S(2)}, u32[]{:S(2)}) collective-permute-start(bf16[3,512,128]{2,1,0:T(8,128)(2,1)S(1)} %copy-done), channel_id=1, source_target_pairs={{0,1},{1,0},{2,3},{3,2},{4,5},{5,4},{6,7},{7,6},{8,9},{9,8},{10,11... | collective-permute-start | bytes 1179656 | tf_op jit(solution)/shard_map/ppermute | solution.py:26
  26.2 16.3 %collective-permute-start.8 = (bf16[3,512,128]{2,1,0:T(8,128)(2,1)S(1)}, bf16[3,512,128]{2,1,0:T(8,128)(2,1)S(1)}, u32[]{:S(2)}, u32[]{:S(2)}) collective-permute-start(bf16[3,512,128]{2,1,0:T(8,128)(2,1)S(1)} %get-tuple-element.46), channel_id=1, source_target_pairs={{0,1},{1,0},{2,3},{3,2},{4,5},{5,4},{6,7},{7,6},{8,9},{9,8},{10,11... | collective-permute-start | bytes 1179656 | tf_op jit(solution)/shard_map/ppermute | solution.py:26
  26.7 11.1 %collective-permute-start.5 = (bf16[2,512,128]{2,1,0:T(8,128)(2,1)S(1)}, bf16[2,512,128]{2,1,0:T(8,128)(2,1)S(1)}, u32[]{:S(2)}, u32[]{:S(2)}) collective-permute-start(bf16[2,512,128]{2,1,0:T(8,128)(2,1)S(1)} %get-tuple-element.41), channel_id=1, source_target_pairs={{8,0},{9,1},{10,2},{11,3},{12,4},{13,5},{14,6},{15,7},{16,8},{17,9... | collective-permute-start | bytes 786440 | tf_op jit(solution)/shard_map/ppermute | solution.py:26
  29.6 12.7 %collective-permute-start.6 = (bf16[2,512,128]{2,1,0:T(8,128)(2,1)S(1)}, bf16[2,512,128]{2,1,0:T(8,128)(2,1)S(1)}, u32[]{:S(2)}, u32[]{:S(2)}) collective-permute-start(bf16[2,512,128]{2,1,0:T(8,128)(2,1)S(1)} %get-tuple-element.42), channel_id=1, source_target_pairs={{8,2},{9,3},{10,0},{11,1},{12,6},{13,7},{14,4},{15,5},{16,10},{17,... | collective-permute-start | bytes 786440 | tf_op jit(solution)/shard_map/ppermute | solution.py:26
  31.0 11.4 %collective-permute-start.4 = (bf16[2,512,128]{2,1,0:T(8,128)(2,1)S(1)}, bf16[2,512,128]{2,1,0:T(8,128)(2,1)S(1)}, u32[]{:S(2)}, u32[]{:S(2)}) collective-permute-start(bf16[2,512,128]{2,1,0:T(8,128)(2,1)S(1)} %shard_map.69), channel_id=1, source_target_pairs={{0,4},{1,5},{2,6},{3,7},{4,8},{5,9},{6,10},{7,11},{8,12},{9,13},{1... | collective-permute-start | bytes 786440 | tf_op jit(solution)/shard_map/ppermute | solution.py:26
  37.7 7.4 %collective-permute-start.12 = (bf16[3,512,128]{2,1,0:T(8,128)(2,1)S(1)}, bf16[3,512,128]{2,1,0:T(8,128)(2,1)S(1)}, u32[]{:S(2)}, u32[]{:S(2)}) collective-permute-start(bf16[3,512,128]{2,1,0:T(8,128)(2,1)S(1)} %collective-permute-done.10.w2_ref), channel_id=1, source_target_pairs={{0,1},{1,0},{2,3},{3,2},{4,5},{5,4},{6,7},{7,6},{8,9},{9,8},{10,11... | collective-permute-start | bytes 1179656 | tf_op jit(solution)/shard_map/ppermute | solution.py:26
  42.4 9.5 %collective-permute-start.7 = (bf16[2,3,256,128]{3,2,1,0:T(8,128)(2,1)S(1)}, bf16[2,3,256,128]{3,2,1,0:T(8,128)(2,1)S(1)}, u32[]{:S(2)}, u32[]{:S(2)}) collective-permute-start(bf16[2,3,256,128]{3,2,1,0:T(8,128)(2,1)S(1)} %get-tuple-element.43), channel_id=1, source_target_pairs={{0,1},{1,0},{2,3},{3,2},{4,5},{5,4},{6,7},{7,6},{8,9},{9,8},{10,11... | collective-permute-start | bytes 1179656 | tf_op jit(solution)/shard_map/ppermute | solution.py:26
  43.1 8.8 %collective-permute-start.11 = (bf16[256,512]{1,0:T(8,128)(2,1)S(1)}, bf16[256,512]{1,0:T(8,128)(2,1)S(1)}, u32[]{:S(2)}, u32[]{:S(2)}) collective-permute-start(bf16[256,512]{1,0:T(8,128)(2,1)S(1)} %get-tuple-element.48), channel_id=1, source_target_pairs={{0,2},{1,3},{2,0},{3,1},{4,6},{5,7},{6,4},{7,5},{8,10},{9,11},{10,... | collective-permute-start | bytes 786440 | tf_op jit(solution)/shard_map/ppermute | solution.py:26

commit v4 on v3

--- a/solution.py
+++ b/solution.py
@@ -191,7 +191,8 @@
 
 
 def near_kernel(
-    lengths_ref, qa_ref, qb_ref, kvn_ref, dq_in, dq_ref, dkn_ref, dvn_ref, *masked
+    lengths_ref, qa_ref, qb_ref, qan_ref, kvn_ref, dq_in, dqa_in,
+    dq_ref, dqa_ref, dkn_ref, dvn_ref, *masked,
 ):
     half, rows = qa_ref.shape[1], kvn_ref.shape[1]
     me = lax.axis_index("seq")
@@ -200,13 +201,15 @@
     query_rows, key_row = pair_limits(lengths_ref, me * rows, (me - 2) * rows, rows)
     for n, (qg_ref, dq) in enumerate(zip((qa_ref, qb_ref), halves(dq_ref))):
         sweep(qg_ref, kvn_ref, dq, dkn_ref, dvn_ref, query_rows - n * half, key_row, 2, *masked)
+    query_rows, key_row = pair_limits(lengths_ref, (me + 1) * rows, (me - 2) * rows, rows)
+    sweep(qan_ref, kvn_ref, dqa_ref, dkn_ref, dvn_ref, query_rows, key_row, 2, *masked)
 
 
 def rest_kernel(
-    lengths_ref, qan_ref, qbn_ref, kv_ref, kvn_ref,
-    dq_ref, dqa_in, dk_in, dv_in, dkn_in, dvn_in,
+    lengths_ref, qbn_ref, kv_ref, kvn_ref,
+    dq_ref, dqa_ref, dk_in, dv_in, dkn_in, dvn_in,
     keep_ref, send_ref, dq_same, dq_cross, dkv_same, dkv_cross,
-    dqa_ref, dk_own, dv_own, dk_ref, dv_ref,
+    dk_own, dv_own, dk_ref, dv_ref,
     dqb_ref, *masked,
 ):
     width = dq_ref.shape[1]
@@ -218,7 +221,6 @@
     sweep(qbn_ref, kv_ref, dqb_ref, dk_own, dv_own, tail_rows, key_row, 2, *masked)
     query_rows, key_row = pair_limits(lengths_ref, (me + 1) * rows, (me - 2) * rows, rows)
     tail_rows = query_rows - rows // 2
-    sweep(qan_ref, kvn_ref, dqa_ref, dk_ref, dv_ref, query_rows, key_row, 2, *masked)
     sweep(qbn_ref, kvn_ref, dqb_ref, dk_ref, dv_ref, tail_rows, key_row, 2, *masked)
 
     norm = MAXLEN**-0.5
@@ -335,9 +337,10 @@
         next_kernel, (half_wide, wide, wide), (lengths, qan, kv, dk, dv), pair_flops,
         scratch=masked, aliases=((3, 1), (4, 2)),
     )
-    dq, dkn, dvn = call(
-        near_kernel, (wide, wide, wide), (lengths, qa, qb, kvn, dq), pair_flops,
-        scratch=masked, aliases=((4, 0),),
+    dq, dqn, dkn, dvn = call(
+        near_kernel, (wide, half_wide, wide, wide),
+        (lengths, qa, qb, qan, kvn, dq, dqn), pair_flops,
+        scratch=masked, aliases=((5, 0), (6, 1)),
     )
     keep, send, dq_same, dq_cross, dkv_same, dkv_cross, *_ = call(
         rest_kernel,
@@ -345,11 +348,11 @@
             like((3, 2 * block, width), BF16), like((3, 2 * block, width), BF16),
             like((2 * block, width), BF16), like((2 * block, width), BF16),
             like((2, 2 * block, width), BF16), like((2, 2 * block, width), BF16),
-            half_wide, wide, wide, wide, wide,
+            wide, wide, wide, wide,
         ),
-        (lengths, qan, qbn, kv, kvn, dq, dqn, dk, dv, dkn, dvn), pair_flops,
+        (lengths, qbn, kv, kvn, dq, dqn, dk, dv, dkn, dvn), pair_flops,
         scratch=[pltpu.VMEM((rows // 2, width), F32), *masked],
-        aliases=((6, 6), (7, 7), (8, 8), (9, 9), (10, 10)),
+        aliases=((6, 6), (7, 7), (8, 8), (9, 9)),
     )
     w1, w3 = shift(w_proj, 0, 1), shift(w2, 0, 1)
     partner = shift(dq_cross, 0, 2)

time: 53.3 us -> 53.3 us (level)
  no operation moved by 1% of the time
where the time goes in v4:
time: 53.3 us; the launch traced here: 53.1 us
  starting transfers between devices  19.7 us (37%)
  waiting for transfers between devices  19.2 us (36%)
  Pallas kernels  14 us (26%)
    ppermute x13, starting transfers between devices, shift(): return lax.ppermute(value, ('seq', 'head'), pairs)  19.7 us
    ppermute x13, waiting for transfers between devices, shift(): return lax.ppermute(value, ('seq', 'head'), pairs)  19.2 us
    pallas_call x10, Pallas kernels, call(): pl.pallas_call(body, out_shape=outs, in_specs=specs, out_specs=tuple((VME...  14 us
  transfers between devices with their start and end apart: 13, of which 6 were waited for; matrix products, arithmetic and copies ran while one was open for 0% of the time, Pallas kernels for 22%

profile of v4, /device:TPU:0, one launch (start us, length us, event | category | flops | bytes accessed | tf_op | source)
XLA Modules:
  0.0 53.1 jit_solution(18417670675016672252)
XLA Ops:
  0.0 0.0 copy-start
  0.0 1.3 %shard_map.64 = (bf16[2,512,128]{2,1,0:T(8,128)(2,1)S(1)}, bf16[2,512,128]{2,1,0:T(8,128)(2,1)S(1)}, bf16[2,1024,128]{2,1,0:T(8,128)(2,1)S(1)}) custom-call(bf16[1024,128]{1,0:T(8,128)(2,1)} %q_hbm.1, bf16[1024,128]{1,0:T(8,128)(2,1)} %g_hbm.1, bf16[1024,128]{1,0:T(8,128)(2,1)} %k_hbm.1, bf16[1024,128]{1,0:T(8,128)(2,1)} %v_hbm.1), custom_call_target="tpu_custom_call" | custom-call | flops 1000 | bytes 2097152 | tf_op jit(solution)/shard_map/pallas_call | solution.py:297
  1.3 5.0 %collective-permute-start.1 = (bf16[2,1024,128]{2,1,0:T(8,128)(2,1)S(1)}, bf16[2,1024,128]{2,1,0:T(8,128)(2,1)S(1)}, u32[]{:S(2)}, u32[]{:S(2)}) collective-permute-start(bf16[2,1024,128]{2,1,0:T(8,128)(2,1)S(1)} %get-tuple-element.29.kv_ref), channel_id=1, source_target_pairs={{0,8},{1,9},{2,10},{3,11},{4,12},{5,13},{6,14},{7,15},{8,16},{9,17... | collective-permute-start | bytes 1572872 | tf_op jit(solution)/shard_map/ppermute | solution.py:26
  6.3 0.0 copy-start.1
  6.3 1.3 %collective-permute-start.2 = (bf16[2,512,128]{2,1,0:T(8,128)(2,1)S(1)}, bf16[2,512,128]{2,1,0:T(8,128)(2,1)S(1)}, u32[]{:S(2)}, u32[]{:S(2)}) collective-permute-start(bf16[2,512,128]{2,1,0:T(8,128)(2,1)S(1)} %get-tuple-element.30.qa_ref), channel_id=1, source_target_pairs={{4,0},{5,1},{6,2},{7,3},{8,4},{9,5},{10,6},{11,7},{12,8},{13,9},{1... | collective-permute-start | bytes 786440 | tf_op jit(solution)/shard_map/ppermute | solution.py:26
  7.6 1.3 %collective-permute-start = (bf16[2,512,128]{2,1,0:T(8,128)(2,1)S(1)}, bf16[2,512,128]{2,1,0:T(8,128)(2,1)S(1)}, u32[]{:S(2)}, u32[]{:S(2)}) collective-permute-start(bf16[2,512,128]{2,1,0:T(8,128)(2,1)S(1)} %get-tuple-element.28.qb_ref), channel_id=1, source_target_pairs={{4,0},{5,1},{6,2},{7,3},{8,4},{9,5},{10,6},{11,7},{12,8},{13,9},{1... | collective-permute-start | bytes 786440 | tf_op jit(solution)/shard_map/ppermute | solution.py:26
  8.9 0.0 copy-done
  8.9 1.6 %collective-permute-start.10 = (bf16[3,512,128]{2,1,0:T(8,128)(2,1)S(1)}, bf16[3,512,128]{2,1,0:T(8,128)(2,1)S(1)}, u32[]{:S(2)}, u32[]{:S(2)}) collective-permute-start(bf16[3,512,128]{2,1,0:T(8,128)(2,1)S(1)} %copy-done), channel_id=1, source_target_pairs={{0,2},{1,3},{2,0},{3,1},{4,6},{5,7},{6,4},{7,5},{8,10},{9,11},{10,... | collective-permute-start | bytes 1179656 | tf_op jit(solution)/shard_map/ppermute | solution.py:26
  10.5 0.0 copy-done.1
  10.5 3.8 %shard_map.65 = (f32[1024,128]{1,0:T(8,128)S(1)}, f32[1024,128]{1,0:T(8,128)S(1)}, f32[1024,128]{1,0:T(8,128)S(1)}) custom-call(s32[4]{0:T(128)S(1)} %copy-done.1, bf16[2,512,128]{2,1,0:T(8,128)(2,1)S(1)} %get-tuple-element.30.qa_ref, bf16[2,512,128]{2,1,0:T(8,128)(2,1)S(1)} %get-tuple-element.28.qb_ref, bf16[2,1024,128]{2,1,0:T(8,128)(2,1)S(1)} %get-tuple-element.29.kv_ref), custom_call_target="tpu_custom_call" | custom-call | flops 1342177280 | bytes 2621456 | tf_op jit(solution)/shard_map/pallas_call | solution.py:297
  14.3 3.1 %collective-permute-done.2.qan_ref = bf16[2,512,128]{2,1,0:T(8,128)(2,1)S(1)} collective-permute-done((bf16[2,512,128]{2,1,0:T(8,128)(2,1)S(1)}, bf16[2,512,128]{2,1,0:T(8,128)(2,1)S(1)}, u32[]{:S(2)}, u32[]{:S(2)}) %collective-permute-start.2) | collective-permute-done | bytes 262176 | tf_op jit(solution)/shard_map/ppermute | solution.py:26
  17.4 2.7 %shard_map.66 = (f32[512,128]{1,0:T(8,128)S(1)}, f32[1024,128]{1,0:T(8,128)S(1)}, f32[1024,128]{1,0:T(8,128)S(1)}) custom-call(s32[4]{0:T(128)S(1)} %copy-done.1, bf16[2,512,128]{2,1,0:T(8,128)(2,1)S(1)} %collective-permute-done.2.qan_ref, bf16[2,1024,128]{2,1,0:T(8,128)(2,1)S(1)} %get-tuple-element.29.kv_ref, ...), custom_call_target="tpu_custom_call", output_to_operand_aliasing={{1}: (3, {}), {2}: (4, {})} | custom-call | flops 1342177280 | bytes 3145744 | tf_op jit(solution)/shard_map/pallas_call | solution.py:297
  20.1 0.0 collective-permute-done.1.kvn_ref
  20.1 0.9 %shard_map.67 = (f32[1024,128]{1,0:T(8,128)S(1)}, f32[512,128]{1,0:T(8,128)S(1)}, f32[1024,128]{1,0:T(8,128)S(1)}, f32[1024,128]{1,0:T(8,128)S(1)}) custom-call(s32[4]{0:T(128)S(1)} %copy-done.1, bf16[2,512,128]{2,1,0:T(8,128)(2,1)S(1)} %get-tuple-element.30.qa_ref, ...), custom_call_target="tpu_custom_call", output_to_operand_aliasing={{0}: (5, {}), {1}: (6, {})} | custom-call | flops 1342177280 | bytes 3932176 | tf_op jit(solution)/shard_map/pallas_call | solution.py:297
  21.0 0.6 %collective-permute-done.qbn_ref = bf16[2,512,128]{2,1,0:T(8,128)(2,1)S(1)} collective-permute-done((bf16[2,512,128]{2,1,0:T(8,128)(2,1)S(1)}, bf16[2,512,128]{2,1,0:T(8,128)(2,1)S(1)}, u32[]{:S(2)}, u32[]{:S(2)}) %collective-permute-start) | collective-permute-done | bytes 262176 | tf_op jit(solution)/shard_map/ppermute | solution.py:26
  21.6 3.0 %shard_map.68 = (bf16[3,512,128]{2,1,0:T(8,128)(2,1)S(1)}, bf16[3,512,128]{2,1,0:T(8,128)(2,1)S(1)}, bf16[512,128]{1,0:T(8,128)(2,1)S(1)}, bf16[512,128]{1,0:T(8...) custom-call(s32[4]{0:T(128)S(1)} %copy-done.1, ...), custom_call_target="tpu_custom_call", output_to_operand_aliasing={{6}: (6, {}), {7}: (7, {}), {8}: (8, {}), {9}: (9, {})} | custom-call | flops 1342177280 | bytes 7864336 | tf_op jit(solution)/shard_map/pallas_call | solution.py:297
  24.6 1.6 %collective-permute-start.3 = (bf16[512,128]{1,0:T(8,128)(2,1)S(1)}, bf16[512,128]{1,0:T(8,128)(2,1)S(1)}, u32[]{:S(2)}, u32[]{:S(2)}) collective-permute-start(bf16[512,128]{1,0:T(8,128)(2,1)S(1)} %get-tuple-element.42), channel_id=1, source_target_pairs={{0,2},{1,3},{2,0},{3,1},{4,6},{5,7},{6,4},{7,5},{8,10},{9,11},{10,... | collective-permute-start | bytes 393224 | tf_op jit(solution)/shard_map/ppermute | solution.py:26
  26.2 0.0 collective-permute-start.9
  26.2 0.5 collective-permute-start.8
  26.7 1.3 %collective-permute-start.5 = (bf16[2,512,128]{2,1,0:T(8,128)(2,1)S(1)}, bf16[2,512,128]{2,1,0:T(8,128)(2,1)S(1)}, u32[]{:S(2)}, u32[]{:S(2)}) collective-permute-start(bf16[2,512,128]{2,1,0:T(8,128)(2,1)S(1)} %get-tuple-element.43), channel_id=1, source_target_pairs={{8,0},{9,1},{10,2},{11,3},{12,4},{13,5},{14,6},{15,7},{16,8},{17,9... | collective-permute-start | bytes 786440 | tf_op jit(solution)/shard_map/ppermute | solution.py:26
  28.0 1.7 %collective-permute-done.3.partner_ref = bf16[512,128]{1,0:T(8,128)(2,1)S(1)} collective-permute-done((bf16[512,128]{1,0:T(8,128)(2,1)S(1)}, bf16[512,128]{1,0:T(8,128)(2,1)S(1)}, u32[]{:S(2)}, u32[]{:S(2)}) %collective-permute-start.3) | collective-permute-done | bytes 131104 | tf_op jit(solution)/shard_map/ppermute | solution.py:26
  29.7 1.3 %collective-permute-start.6 = (bf16[2,512,128]{2,1,0:T(8,128)(2,1)S(1)}, bf16[2,512,128]{2,1,0:T(8,128)(2,1)S(1)}, u32[]{:S(2)}, u32[]{:S(2)}) collective-permute-start(bf16[2,512,128]{2,1,0:T(8,128)(2,1)S(1)} %get-tuple-element.44), channel_id=1, source_target_pairs={{8,2},{9,3},{10,0},{11,1},{12,6},{13,7},{14,4},{15,5},{16,10},{17,... | collective-permute-start | bytes 786440 | tf_op jit(solution)/shard_map/ppermute | solution.py:26
  31.0 0.0 collective-permute-done.10.w2_ref
  31.0 4.3 %collective-permute-start.4 = (bf16[2,512,128]{2,1,0:T(8,128)(2,1)S(1)}, bf16[2,512,128]{2,1,0:T(8,128)(2,1)S(1)}, u32[]{:S(2)}, u32[]{:S(2)}) collective-permute-start(bf16[2,512,128]{2,1,0:T(8,128)(2,1)S(1)} %shard_map.69), channel_id=1, source_target_pairs={{0,4},{1,5},{2,6},{3,7},{4,8},{5,9},{6,10},{7,11},{8,12},{9,13},{1... | collective-permute-start | bytes 786440 | tf_op jit(solution)/shard_map/ppermute | solution.py:26
  35.3 2.4 %collective-permute-done.5.dkv_same = bf16[2,512,128]{2,1,0:T(8,128)(2,1)S(1)} collective-permute-done((bf16[2,512,128]{2,1,0:T(8,128)(2,1)S(1)}, bf16[2,512,128]{2,1,0:T(8,128)(2,1)S(1)}, u32[]{:S(2)}, u32[]{:S(2)}) %collective-permute-start.5) | collective-permute-done | bytes 262176 | tf_op jit(solution)/shard_map/ppermute | solution.py:26
  37.7 0.0 collective-permute-start.12
  37.8 4.6 %collective-permute-done.6.dkv_cross = bf16[2,512,128]{2,1,0:T(8,128)(2,1)S(1)} collective-permute-done((bf16[2,512,128]{2,1,0:T(8,128)(2,1)S(1)}, bf16[2,512,128]{2,1,0:T(8,128)(2,1)S(1)}, u32[]{:S(2)}, u32[]{:S(2)}) %collective-permute-start.6) | collective-permute-done | bytes 262176 | tf_op jit(solution)/shard_map/ppermute | solution.py:26
  42.4 0.0 collective-permute-done.4.dq_pair
  42.4 0.1 shard_map.70
  42.4 0.1 collective-permute-start.7
  42.5 0.0 collective-permute-done.9.w1_ref
  42.5 0.0 collective-permute-done.8.got_ref
  42.5 0.6 %shard_map.71 = (f32[256,512]{1,0:T(8,128)S(1)}, bf16[256,512]{1,0:T(8,128)(2,1)S(1)}) custom-call(bf16[3,512,128]{2,1,0:T(8,128)(2,1)S(1)} %get-tuple-element.47.keep_ref, bf16[3,512,128]{2,1,0:T(8,128)(2,1)S(1)} %collective-permute-done.8.got_ref, bf16[3,512,128]{2,1,0:T(8,128)(2,1)S(1)} %copy-done, bf16[3,512,128]{2,1,0:T(8,128)(2,1)S(1)} %collective-permute-done.9.w1_ref), custom_call_target="tpu_custom_call" | custom-call | flops 201326592 | bytes 2359296 | tf_op jit(solution)/shard_map/pallas_call | solution.py:297
  43.1 1.6 %collective-permute-start.11 = (bf16[256,512]{1,0:T(8,128)(2,1)S(1)}, bf16[256,512]{1,0:T(8,128)(2,1)S(1)}, u32[]{:S(2)}, u32[]{:S(2)}) collective-permute-start(bf16[256,512]{1,0:T(8,128)(2,1)S(1)} %get-tuple-element.50), channel_id=1, source_target_pairs={{0,2},{1,3},{2,0},{3,1},{4,6},{5,7},{6,4},{7,5},{8,10},{9,11},{10,... | collective-permute-start | bytes 786440 | tf_op jit(solution)/shard_map/ppermute | solution.py:26
  44.7 0.4 shard_map.72.partial_ref
  45.1 0.0 collective-permute-done.12.w3_ref
  45.1 6.8 %collective-permute-done.11.arrived_ref = bf16[256,512]{1,0:T(8,128)(2,1)S(1)} collective-permute-done((bf16[256,512]{1,0:T(8,128)(2,1)S(1)}, bf16[256,512]{1,0:T(8,128)(2,1)S(1)}, u32[]{:S(2)}, u32[]{:S(2)}) %collective-permute-start.11) | collective-permute-done | bytes 262176 | tf_op jit(solution)/shard_map/ppermute | solution.py:26
  51.9 0.0 collective-permute-done.7.got_ref
  51.9 1.2 %shard_map.73 = f32[256,512]{1,0:T(8,128)} custom-call(bf16[2,3,256,128]{3,2,1,0:T(8,128)(2,1)S(1)} %collective-permute-done.7.got_ref, f32[256,512]{1,0:T(8,128)S(1)} %shard_map.72.partial_ref, bf16[256,512]{1,0:T(8,128)(2,1)S(1)} %collective-permute-done.11.arrived_ref, bf16[3,512,128]{2,1,0:T(8,128)(2,1)S(1)} %collective-permute-done.9.w1_ref, ...), custom_call_target="tpu_custom_call" | custom-call | flops 201326592 | bytes 2490368 | tf_op jit(solution)/shard_map/pallas_call | solution.py:297
  (1 shorter events, 0.0 us)
Async XLA Ops:
  0.0 8.9 %copy-start = (bf16[3,512,128]{2,1,0:T(8,128)(2,1)S(1)}, bf16[3,512,128]{2,1,0:T(8,128)(2,1)}, u32[]{:S(2)}) copy-start(bf16[3,512,128]{2,1,0:T(8,128)(2,1)} %w_ref.3) | copy-start | bytes 1179652
  1.3 18.8 %collective-permute-start.1 = (bf16[2,1024,128]{2,1,0:T(8,128)(2,1)S(1)}, bf16[2,1024,128]{2,1,0:T(8,128)(2,1)S(1)}, u32[]{:S(2)}, u32[]{:S(2)}) collective-permute-start(bf16[2,1024,128]{2,1,0:T(8,128)(2,1)S(1)} %get-tuple-element.29.kv_ref), channel_id=1, source_target_pairs={{0,8},{1,9},{2,10},{3,11},{4,12},{5,13},{6,14},{7,15},{8,16},{9,17... | collective-permute-start | bytes 1572872 | tf_op jit(solution)/shard_map/ppermute | solution.py:26
  6.3 4.2 %copy-start.1 = (s32[4]{0:T(128)S(1)}, s32[4]{0:T(128)}, u32[]{:S(2)}) copy-start(s32[4]{0:T(128)} %lengths_ref.7) | copy-start | bytes 52
  6.3 11.1 %collective-permute-start.2 = (bf16[2,512,128]{2,1,0:T(8,128)(2,1)S(1)}, bf16[2,512,128]{2,1,0:T(8,128)(2,1)S(1)}, u32[]{:S(2)}, u32[]{:S(2)}) collective-permute-start(bf16[2,512,128]{2,1,0:T(8,128)(2,1)S(1)} %get-tuple-element.30.qa_ref), channel_id=1, source_target_pairs={{4,0},{5,1},{6,2},{7,3},{8,4},{9,5},{10,6},{11,7},{12,8},{13,9},{1... | collective-permute-start | bytes 786440 | tf_op jit(solution)/shard_map/ppermute | solution.py:26
  7.6 14.0 %collective-permute-start = (bf16[2,512,128]{2,1,0:T(8,128)(2,1)S(1)}, bf16[2,512,128]{2,1,0:T(8,128)(2,1)S(1)}, u32[]{:S(2)}, u32[]{:S(2)}) collective-permute-start(bf16[2,512,128]{2,1,0:T(8,128)(2,1)S(1)} %get-tuple-element.28.qb_ref), channel_id=1, source_target_pairs={{4,0},{5,1},{6,2},{7,3},{8,4},{9,5},{10,6},{11,7},{12,8},{13,9},{1... | collective-permute-start | bytes 786440 | tf_op jit(solution)/shard_map/ppermute | solution.py:26
  8.9 22.1 %collective-permute-start.10 = (bf16[3,512,128]{2,1,0:T(8,128)(2,1)S(1)}, bf16[3,512,128]{2,1,0:T(8,128)(2,1)S(1)}, u32[]{:S(2)}, u32[]{:S(2)}) collective-permute-start(bf16[3,512,128]{2,1,0:T(8,128)(2,1)S(1)} %copy-done), channel_id=1, source_target_pairs={{0,2},{1,3},{2,0},{3,1},{4,6},{5,7},{6,4},{7,5},{8,10},{9,11},{10,... | collective-permute-start | bytes 1179656 | tf_op jit(solution)/shard_map/ppermute | solution.py:26
  24.6 5.0 %collective-permute-start.3 = (bf16[512,128]{1,0:T(8,128)(2,1)S(1)}, bf16[512,128]{1,0:T(8,128)(2,1)S(1)}, u32[]{:S(2)}, u32[]{:S(2)}) collective-permute-start(bf16[512,128]{1,0:T(8,128)(2,1)S(1)} %get-tuple-element.42), channel_id=1, source_target_pairs={{0,2},{1,3},{2,0},{3,1},{4,6},{5,7},{6,4},{7,5},{8,10},{9,11},{10,... | collective-permute-start | bytes 393224 | tf_op jit(solution)/shard_map/ppermute | solution.py:26
  26.2 16.3 %collective-permute-start.9 = (bf16[3,512,128]{2,1,0:T(8,128)(2,1)S(1)}, bf16[3,512,128]{2,1,0:T(8,128)(2,1)S(1)}, u32[]{:S(2)}, u32[]{:S(2)}) collective-permute-start(bf16[3,512,128]{2,1,0:T(8,128)(2,1)S(1)} %copy-done), channel_id=1, source_target_pairs={{0,1},{1,0},{2,3},{3,2},{4,5},{5,4},{6,7},{7,6},{8,9},{9,8},{10,11... | collective-permute-start | bytes 1179656 | tf_op jit(solution)/shard_map/ppermute | solution.py:26
  26.2 16.3 %collective-permute-start.8 = (bf16[3,512,128]{2,1,0:T(8,128)(2,1)S(1)}, bf16[3,512,128]{2,1,0:T(8,128)(2,1)S(1)}, u32[]{:S(2)}, u32[]{:S(2)}) collective-permute-start(bf16[3,512,128]{2,1,0:T(8,128)(2,1)S(1)} %get-tuple-element.48), channel_id=1, source_target_pairs={{0,1},{1,0},{2,3},{3,2},{4,5},{5,4},{6,7},{7,6},{8,9},{9,8},{10,11... | collective-permute-start | bytes 1179656 | tf_op jit(solution)/shard_map/ppermute | solution.py:26
  26.7 11.1 %collective-permute-start.5 = (bf16[2,512,128]{2,1,0:T(8,128)(2,1)S(1)}, bf16[2,512,128]{2,1,0:T(8,128)(2,1)S(1)}, u32[]{:S(2)}, u32[]{:S(2)}) collective-permute-start(bf16[2,512,128]{2,1,0:T(8,128)(2,1)S(1)} %get-tuple-element.43), channel_id=1, source_target_pairs={{8,0},{9,1},{10,2},{11,3},{12,4},{13,5},{14,6},{15,7},{16,8},{17,9... | collective-permute-start | bytes 786440 | tf_op jit(solution)/shard_map/ppermute | solution.py:26
  29.7 12.7 %collective-permute-start.6 = (bf16[2,512,128]{2,1,0:T(8,128)(2,1)S(1)}, bf16[2,512,128]{2,1,0:T(8,128)(2,1)S(1)}, u32[]{:S(2)}, u32[]{:S(2)}) collective-permute-start(bf16[2,512,128]{2,1,0:T(8,128)(2,1)S(1)} %get-tuple-element.44), channel_id=1, source_target_pairs={{8,2},{9,3},{10,0},{11,1},{12,6},{13,7},{14,4},{15,5},{16,10},{17,... | collective-permute-start | bytes 786440 | tf_op jit(solution)/shard_map/ppermute | solution.py:26
  31.0 11.4 %collective-permute-start.4 = (bf16[2,512,128]{2,1,0:T(8,128)(2,1)S(1)}, bf16[2,512,128]{2,1,0:T(8,128)(2,1)S(1)}, u32[]{:S(2)}, u32[]{:S(2)}) collective-permute-start(bf16[2,512,128]{2,1,0:T(8,128)(2,1)S(1)} %shard_map.69), channel_id=1, source_target_pairs={{0,4},{1,5},{2,6},{3,7},{4,8},{5,9},{6,10},{7,11},{8,12},{9,13},{1... | collective-permute-start | bytes 786440 | tf_op jit(solution)/shard_map/ppermute | solution.py:26
  37.7 7.4 %collective-permute-start.12 = (bf16[3,512,128]{2,1,0:T(8,128)(2,1)S(1)}, bf16[3,512,128]{2,1,0:T(8,128)(2,1)S(1)}, u32[]{:S(2)}, u32[]{:S(2)}) collective-permute-start(bf16[3,512,128]{2,1,0:T(8,128)(2,1)S(1)} %collective-permute-done.10.w2_ref), channel_id=1, source_target_pairs={{0,1},{1,0},{2,3},{3,2},{4,5},{5,4},{6,7},{7,6},{8,9},{9,8},{10,11... | collective-permute-start | bytes 1179656 | tf_op jit(solution)/shard_map/ppermute | solution.py:26
  42.4 9.5 %collective-permute-start.7 = (bf16[2,3,256,128]{3,2,1,0:T(8,128)(2,1)S(1)}, bf16[2,3,256,128]{3,2,1,0:T(8,128)(2,1)S(1)}, u32[]{:S(2)}, u32[]{:S(2)}) collective-permute-start(bf16[2,3,256,128]{3,2,1,0:T(8,128)(2,1)S(1)} %get-tuple-element.45), channel_id=1, source_target_pairs={{0,1},{1,0},{2,3},{3,2},{4,5},{5,4},{6,7},{7,6},{8,9},{9,8},{10,11... | collective-permute-start | bytes 1179656 | tf_op jit(solution)/shard_map/ppermute | solution.py:26
  43.1 8.8 %collective-permute-start.11 = (bf16[256,512]{1,0:T(8,128)(2,1)S(1)}, bf16[256,512]{1,0:T(8,128)(2,1)S(1)}, u32[]{:S(2)}, u32[]{:S(2)}) collective-permute-start(bf16[256,512]{1,0:T(8,128)(2,1)S(1)} %get-tuple-element.50), channel_id=1, source_target_pairs={{0,2},{1,3},{2,0},{3,1},{4,6},{5,7},{6,4},{7,5},{8,10},{9,11},{10,... | collective-permute-start | bytes 786440 | tf_op jit(solution)/shard_map/ppermute | solution.py:26
